TPU v7x, 32 devices: a whole 2x2x4 slice. The times are simulated.
32 devices in a mesh: dp: 8 (over y, x, core), tensor: 4 (over z).
Axes of the slice: x: 2, y: 2, z: 4, core: 2. Of those that a mesh axis runs over, the one named last changes fastest.
Arguments:
- tokens: bfloat16 [16384, 1024], P(('dp', 'tensor')), may hold values from -6 to 6
- lengths: int32 [32], P('dp'), may hold values from 1 to 512, 10240 in all
- w_qkv: bfloat16 [1024, 3, 1024], P('dp', None, 'tensor'), may hold values from -0.1875 to 0.1875
- b_qv: bfloat16 [2, 1024], P(None, 'tensor'), may hold values from -3 to 3
- w_out: bfloat16 [1024, 1024], P('dp', 'tensor'), may hold values from -1 to 1
- b_out: bfloat16 [1024], replicated, may hold values from -3 to 3
- gain_one: bfloat16 [1024], replicated, may hold values from 0.5 to 1.5
- shift_one: bfloat16 [1024], replicated, may hold values from -3 to 3
- w_in: bfloat16 [1024, 4096], P('dp', 'tensor'), may hold values from -0.1875 to 0.1875
- b_in: bfloat16 [4096], P('tensor'), may hold values from -3 to 3
- w_back: bfloat16 [1024, 4096], P('dp', 'tensor'), may hold values from -0.09375 to 0.09375
- b_back: bfloat16 [1024], replicated, may hold values from -3 to 3
- gain_two: bfloat16 [1024], replicated, may hold values from 0.5 to 1.5
- shift_two: bfloat16 [1024], replicated, may hold values from -3 to 3
- cotangent: bfloat16 [16384, 1024], P(('dp', 'tensor')), may hold values from -6 to 6
Outputs:
- output: bfloat16 [16384, 1024], P(('dp', 'tensor'))
- grad_tokens: float32 [16384, 1024], P(('dp', 'tensor'))
- grad_w_qkv: float32 [1024, 3, 1024], P('dp', None, 'tensor')
- grad_b_qv: float32 [2, 1024], P(None, 'tensor')
- grad_w_out: float32 [1024, 1024], P('dp', 'tensor')
- grad_b_out: float32 [1024], replicated
- grad_gain_one: float32 [1024], replicated
- grad_shift_one: float32 [1024], replicated
- grad_w_in: float32 [1024, 4096], P('dp', 'tensor')
- grad_b_in: float32 [4096], P('tensor')
- grad_w_back: float32 [1024, 4096], P('dp', 'tensor')
- grad_b_back: float32 [1024], replicated
- grad_gain_two: float32 [1024], replicated
- grad_shift_two: float32 [1024], replicated
Inputs may be any that keep to these rules, and one draw needn't show every extreme that they name: `lengths`: the valid tokens of each sequence; all of them sum to 10240 and the largest is 512.
All inputs are finite; a program needn't handle non-finite values. No bound on the sum of `lengths` on one device may be relied on, other than what follows from the above.
Results may differ from a plain program's by a relative error of at most 0.018.
Values may be sent and summed in bfloat16 or wider, within the bound.
A program may use at most 128 MiB of HBM per device.

v0:
```python
import jax
import jax.numpy as jnp
from jax import lax
from jax.sharding import PartitionSpec as P

H = 16
FF = 4096


EPS = 1e-05
MASKED = -1000000000.0
SQRT_HALF = 0.7071067811865476
INV_ROOT_TAU = 0.3989422804014327
CONTRACT_LAST = (((1,), (1,)), ((), ()))
CONTRACT_FIRST = (((0,), (0,)), ((), ()))


def normalize(values, gain, shift):
    centre = values - jnp.mean(values, axis=-1, keepdims=True)
    inverse = lax.rsqrt(jnp.mean(centre * centre, axis=-1, keepdims=True) + EPS)
    scaled = centre * inverse
    return (scaled * gain + shift, scaled, inverse)


def norm_back(grad_out, scaled, inverse, gain):
    grad_scaled = grad_out * gain
    inner = jnp.mean(grad_scaled, axis=-1, keepdims=True)
    along = jnp.mean(grad_scaled * scaled, axis=-1, keepdims=True)
    return inverse * (grad_scaled - inner - scaled * along)


def body(
    tokens,
    lengths,
    w_qkv,
    b_qv,
    w_out,
    b_out,
    gain_one,
    shift_one,
    w_in,
    b_in,
    w_back,
    b_back,
    gain_two,
    shift_two,
    cotangent,
):
    local_rows = tokens.shape[0]
    width = tokens.shape[1]
    seq_count = lengths.shape[0]
    group_rows = local_rows * lax.axis_size("tensor")
    seq_len = group_rows // seq_count
    local_width = w_qkv.shape[2]
    local_hidden = w_in.shape[1]
    head_dim = width // H
    local_heads = local_width // head_dim
    scale = head_dim ** (-0.5)
    shape4 = (seq_count, seq_len, local_heads, head_dim)
    keep_mask = jnp.arange(seq_len, dtype=jnp.int32)[None, :] < lengths[:, None]
    full_qkv, full_out, full_in, full_back = (
        lax.all_gather(w_qkv, "dp", axis=0, tiled=True),
        lax.all_gather(w_out, "dp", axis=0, tiled=True),
        lax.all_gather(w_in, "dp", axis=0, tiled=True),
        lax.all_gather(w_back, "dp", axis=0, tiled=True),
    )
    gathered = lax.all_gather(tokens, "tensor", axis=0, tiled=True)
    projected = jnp.einsum("rd,dcf->rcf", gathered, full_qkv, preferred_element_type=jnp.float32)
    bias_qv = b_qv.astype(jnp.float32)
    query_rows = (projected[:, 0] + bias_qv[0]).astype(jnp.bfloat16).reshape(shape4)
    key_rows = projected[:, 1].astype(jnp.bfloat16).reshape(shape4)
    value_rows = (projected[:, 2] + bias_qv[1]).astype(jnp.bfloat16).reshape(shape4)

    def masked_scores(query_seq, key_seq, keep):
        scores = (
            jnp.einsum("qhe,khe->hqk", query_seq, key_seq, preferred_element_type=jnp.float32)
            * scale
        )
        return jnp.where(keep[None, None, :], scores, MASKED)

    def attend_one(inputs):
        query_seq, key_seq, value_seq, keep = inputs
        scores = masked_scores(query_seq, key_seq, keep)
        top = jnp.max(scores, axis=-1, keepdims=True)
        expo = jnp.exp(scores - top)
        total = jnp.sum(expo, axis=-1, keepdims=True)
        probs = (expo / total).astype(jnp.bfloat16)
        mixed = jnp.einsum("hqk,khe->qhe", probs, value_seq, preferred_element_type=jnp.float32)
        return (mixed.astype(jnp.bfloat16), top[..., 0] + jnp.log(total[..., 0]))

    mixed_all, log_norm = lax.map(attend_one, (query_rows, key_rows, value_rows, keep_mask))
    attended = mixed_all.reshape(group_rows, local_width)
    rows = attended
    attn_local = lax.psum_scatter(
        lax.dot_general(rows, full_out, CONTRACT_LAST, preferred_element_type=jnp.float32).astype(
            jnp.bfloat16
        ),
        "tensor",
        scatter_dimension=0,
        tiled=True,
    ).astype(jnp.float32)
    residual_one = tokens.astype(jnp.float32) + attn_local + b_out.astype(jnp.float32)
    gain_a = gain_one.astype(jnp.float32)
    hidden, scaled_one, inverse_one = normalize(residual_one, gain_a, shift_one.astype(jnp.float32))
    hidden_all = lax.all_gather(hidden.astype(jnp.bfloat16), "tensor", axis=0, tiled=True)
    pre_act = jnp.dot(hidden_all, full_in, preferred_element_type=jnp.float32) + b_in.astype(
        jnp.float32
    )
    activated = jax.nn.gelu(pre_act, approximate=False).astype(jnp.bfloat16)
    rows = activated
    ffn_local = lax.psum_scatter(
        lax.dot_general(rows, full_back, CONTRACT_LAST, preferred_element_type=jnp.float32).astype(
            jnp.bfloat16
        ),
        "tensor",
        scatter_dimension=0,
        tiled=True,
    ).astype(jnp.float32)
    residual_two = hidden + ffn_local + b_back.astype(jnp.float32)
    gain_b = gain_two.astype(jnp.float32)
    output, scaled_two, inverse_two = normalize(residual_two, gain_b, shift_two.astype(jnp.float32))
    grad_out = cotangent.astype(jnp.float32)
    grad_gain_two = jnp.sum(grad_out * scaled_two, axis=0)
    grad_shift_two = jnp.sum(grad_out, axis=0)
    grad_res_two = norm_back(grad_out, scaled_two, inverse_two, gain_b)
    grad_ffn = grad_res_two.astype(jnp.bfloat16)
    grad_b_back = jnp.sum(grad_ffn.astype(jnp.float32), axis=0)
    back_qkv, back_out, back_in, back_back = (
        lax.all_gather(w_qkv, "dp", axis=0, tiled=True),
        lax.all_gather(w_out, "dp", axis=0, tiled=True),
        lax.all_gather(w_in, "dp", axis=0, tiled=True),
        lax.all_gather(w_back, "dp", axis=0, tiled=True),
    )
    grad_ffn_all = lax.all_gather(grad_ffn, "tensor", axis=0, tiled=True)
    grad_act = jnp.dot(grad_ffn_all, back_back, preferred_element_type=jnp.float32)
    grad_w_back = lax.dot_general(
        grad_ffn_all, activated, CONTRACT_FIRST, preferred_element_type=jnp.float32
    )
    slope = 0.5 * (1.0 + lax.erf(pre_act * SQRT_HALF)) + pre_act * INV_ROOT_TAU * jnp.exp(
        -0.5 * pre_act * pre_act
    )
    grad_pre = (grad_act * slope).astype(jnp.bfloat16)
    grad_b_in = jnp.sum(grad_pre.astype(jnp.float32), axis=0)
    grad_w_in = lax.dot_general(
        hidden_all, grad_pre, CONTRACT_FIRST, preferred_element_type=jnp.float32
    )
    rows = grad_pre
    grad_hidden = (
        lax.psum_scatter(
            lax.dot_general(
                rows, back_in, CONTRACT_LAST, preferred_element_type=jnp.float32
            ).astype(jnp.bfloat16),
            "tensor",
            scatter_dimension=0,
            tiled=True,
        ).astype(jnp.float32)
        + grad_res_two
    )
    grad_gain_one = jnp.sum(grad_hidden * scaled_one, axis=0)
    grad_shift_one = jnp.sum(grad_hidden, axis=0)
    grad_res_one = norm_back(grad_hidden, scaled_one, inverse_one, gain_a)
    grad_attn = grad_res_one.astype(jnp.bfloat16)
    grad_b_out = jnp.sum(grad_attn.astype(jnp.float32), axis=0)
    grad_attn_all = lax.all_gather(grad_attn, "tensor", axis=0, tiled=True)
    grad_mixed = jnp.dot(grad_attn_all, back_out, preferred_element_type=jnp.float32).astype(
        jnp.bfloat16
    )
    grad_w_out = lax.dot_general(
        grad_attn_all, attended, CONTRACT_FIRST, preferred_element_type=jnp.float32
    )

    def attend_back(inputs):
        query_seq, key_seq, value_seq, keep, log_seq, grad_seq = inputs
        scores = masked_scores(query_seq, key_seq, keep)
        probs = jnp.exp(scores - log_seq[..., None])
        grad_probs = jnp.einsum(
            "qhe,khe->hqk", grad_seq, value_seq, preferred_element_type=jnp.float32
        )
        inner = jnp.sum(grad_probs * probs, axis=-1, keepdims=True)
        grad_scores = (probs * (grad_probs - inner)).astype(jnp.bfloat16)
        grad_query = (
            jnp.einsum("hqk,khe->qhe", grad_scores, key_seq, preferred_element_type=jnp.float32)
            * scale
        ).astype(jnp.bfloat16)
        grad_key = (
            jnp.einsum("hqk,qhe->khe", grad_scores, query_seq, preferred_element_type=jnp.float32)
            * scale
        ).astype(jnp.bfloat16)
        grad_value = jnp.einsum(
            "hqk,qhe->khe", probs.astype(jnp.bfloat16), grad_seq, preferred_element_type=jnp.float32
        ).astype(jnp.bfloat16)
        return (grad_query, grad_key, grad_value)

    grad_query, grad_key, grad_value = lax.map(
        attend_back,
        (query_rows, key_rows, value_rows, keep_mask, log_norm, grad_mixed.reshape(shape4)),
    )
    grad_qkv = jnp.stack(
        [
            grad_query.reshape(group_rows, local_width),
            grad_key.reshape(group_rows, local_width),
            grad_value.reshape(group_rows, local_width),
        ],
        axis=1,
    )
    grad_b_qv = jnp.stack(
        [
            jnp.sum(grad_qkv[:, 0].astype(jnp.float32), axis=0),
            jnp.sum(grad_qkv[:, 2].astype(jnp.float32), axis=0),
        ],
        axis=0,
    )
    grad_w_qkv = jnp.einsum("rd,rcf->dcf", gathered, grad_qkv, preferred_element_type=jnp.float32)
    rows = grad_qkv
    grad_tokens = (
        lax.psum_scatter(
            jnp.einsum("rcf,dcf->rd", rows, back_qkv, preferred_element_type=jnp.float32).astype(
                jnp.bfloat16
            ),
            "tensor",
            scatter_dimension=0,
            tiled=True,
        ).astype(jnp.float32)
        + grad_res_one
    )
    owner_qkv, owner_out, owner_in, owner_back = (
        lax.psum_scatter(grad_w_qkv, "dp", scatter_dimension=0, tiled=True),
        lax.psum_scatter(grad_w_out, "dp", scatter_dimension=0, tiled=True),
        lax.psum_scatter(grad_w_in, "dp", scatter_dimension=0, tiled=True),
        lax.psum_scatter(grad_w_back, "dp", scatter_dimension=0, tiled=True),
    )
    slot = lax.axis_index("tensor")
    wide_qv = lax.dynamic_update_slice_in_dim(
        jnp.zeros((2, width), jnp.float32), grad_b_qv, slot * local_width, 1
    )
    wide_in = lax.dynamic_update_slice_in_dim(
        jnp.zeros((FF,), jnp.float32), grad_b_in, slot * local_hidden, 0
    )
    summed = lax.psum(
        (
            wide_qv,
            wide_in,
            grad_b_out,
            grad_gain_one,
            grad_shift_one,
            grad_b_back,
            grad_gain_two,
            grad_shift_two,
        ),
        ("dp", "tensor"),
    )
    owner_b_qv = lax.dynamic_slice_in_dim(summed[0], slot * local_width, local_width, 1)
    owner_b_in = lax.dynamic_slice_in_dim(summed[1], slot * local_hidden, local_hidden, 0)
    return (
        output.astype(jnp.bfloat16),
        grad_tokens,
        owner_qkv,
        owner_b_qv,
        owner_out,
        summed[2],
        summed[3],
        summed[4],
        owner_in,
        owner_b_in,
        owner_back,
        summed[5],
        summed[6],
        summed[7],
    )


def solution(mesh):
    in_specs = (
        P(("dp", "tensor"), None),
        P("dp"),
        P("dp", None, "tensor"),
        P(None, "tensor"),
        P("dp", "tensor"),
        P(),
        P(),
        P(),
        P("dp", "tensor"),
        P("tensor"),
        P("dp", "tensor"),
        P(),
        P(),
        P(),
        P(("dp", "tensor"), None),
    )
    out_specs = (
        P(("dp", "tensor"), None),
        P(("dp", "tensor"), None),
        P("dp", None, "tensor"),
        P(None, "tensor"),
        P("dp", "tensor"),
        P(),
        P(),
        P(),
        P("dp", "tensor"),
        P("tensor"),
        P("dp", "tensor"),
        P(),
        P(),
        P(),
    )
    return jax.shard_map(body, mesh=mesh, in_specs=in_specs, out_specs=out_specs, check_vma=False)
```

profile of v0, /device:TPU:0, one launch (start us, length us, event | category | flops | bytes accessed | tf_op | source)
XLA Modules:
  0.0 1103.4 jit_solution(2574607224132808379)
XLA Ops:
  9.6 13.2 %all_gather.30 = bf16[1024,256]{1,0:T(8,128)(2,1)} all-gather(bf16[128,256]{1,0:T(8,128)(2,1)} %param.23), channel_id=1, replica_groups=mesh['dp'=8,'tensor'=4] {'dp'}, dimensions={0}, use_global_device_ids=true | all-gather | bytes 589824 | tf_op jit(solution)/shard_map/all_gather | solution.py:63
  23.5 14.8 %all-gather.10.cloned.1.call-done = bf16[1024,3,256]{2,0,1:T(8,128)(2,1)} async-done(((bf16[128,3,256]{2,0,1:T(8,128)(2,1)}), bf16[1024,3,256]{2,0,1:T(8,128)(2,1)}) %all-gather.10.cloned.1.call-update) | async-done | bytes 1572880 | tf_op jit(solution)/shard_map/all_gather | solution.py:62
  38.3 82.4 %all-gather.8.cloned.1.call-done = bf16[2048,1024]{1,0:T(8,128)(2,1)} async-done(((bf16[512,1024]{1,0:T(8,128)(2,1)}), bf16[2048,1024]{1,0:T(8,128)(2,1)}) %all-gather.8.cloned.1.call-update) | async-done | bytes 4194320 | tf_op jit(solution)/shard_map/all_gather | solution.py:67
  145.5 16.7 %while.26 = (s32[]{:T(128)}, bf16[4,512,4,64]{1,3,2,0:T(8,128)(2,1)S(1)}, f32[4,4,512]{2,1,0:T(4,128)S(1)}, bf16[4,512,4,64]{1,3,2,0:T(8,128)(2,1)}, pred[4,512]...) while((s32[]{:T(128)}, ...), condition=%wide.region_3.4_spmd, body=%wide.region_0.3_spmd.sunk | while | flops 281147392 | bytes 13701725 | solution.py:91
  168.5 74.6 %reduce-scatter.9.cloned.1.call-done = bf16[512,1024]{1,0:T(8,128)(2,1)} async-done(((bf16[2048,1024]{1,0:T(8,128)(2,1)}), bf16[512,1024]{1,0:T(8,128)(2,1)}) %reduce-scatter.9.cloned.1.call-update) | async-done | bytes 1048592 | tf_op jit(solution)/shard_map/reduce_scatter | solution.py:94
  248.8 24.5 %all-gather.14.cloned.1.call-done = bf16[1024,1024]{1,0:T(8,128)(2,1)} async-done(((bf16[128,1024]{1,0:T(8,128)(2,1)}), bf16[1024,1024]{1,0:T(8,128)(2,1)}) %all-gather.14.cloned.1.call-update) | async-done | bytes 2097168 | tf_op jit(solution)/shard_map/all_gather | solution.py:64
  273.4 82.9 %all-gather.12.cloned.1.call-done = bf16[2048,1024]{1,0:T(8,128)(2,1)} async-done(((bf16[512,1024]{1,0:T(8,128)(2,1)}), bf16[2048,1024]{1,0:T(8,128)(2,1)}) %all-gather.12.cloned.1.call-update) | async-done | bytes 4194320 | tf_op jit(solution)/shard_map/all_gather | solution.py:105
  356.2 25.7 %fusion.61 = (bf16[2048,1024]{1,0:T(8,128)(2,1)}, f32[2048,1024]{1,0:T(8,128)}) fusion(f32[1024]{0:T(1024)S(1)} %convert_element_type.149, bf16[2048,1024]{1,0:T(8,128)(2,1)} %all-gather.12.cloned.1.call-done, bf16[1024,1024]{1,0:T(8,128)(2,1)} %all-gather.14.cloned.1.call-done), kind=kOutput, calls=%fused_computation.68 | convolution fusion | flops 4433379328 | bytes 18878464 | tf_op jit(solution)/shard_map/dot_general | solution.py:106
  384.6 9.4 convolution_convert_fusion.2
  394.7 76.2 %reduce-scatter.11.cloned.1.call-done = bf16[512,1024]{1,0:T(8,128)(2,1)} async-done(((bf16[2048,1024]{1,0:T(8,128)(2,1)}), bf16[512,1024]{1,0:T(8,128)(2,1)}) %reduce-scatter.11.cloned.1.call-update) | async-done | bytes 1048592 | tf_op jit(solution)/shard_map/reduce_scatter | solution.py:111
  477.7 81.4 %all-gather.18.cloned.1.call-done = bf16[2048,1024]{1,0:T(8,128)(2,1)} async-done(((bf16[512,1024]{1,0:T(8,128)(2,1)}), bf16[2048,1024]{1,0:T(8,128)(2,1)}) %all-gather.18.cloned.1.call-update) | async-done | bytes 4194320 | tf_op jit(solution)/shard_map/all_gather | solution.py:134
  559.1 11.3 %convert_reduce_fusion = (f32[1024]{0:T(1024)S(1)}, bf16[2048,1024]{1,0:T(8,128)(2,1)S(1)}) fusion(f32[2048,1024]{1,0:T(8,128)} %get-tuple-element.241, f32[1024]{0:T(1024)S(1)} %convert_element_type.149, bf16[2048,1024]{1,0:T(8,128)(2,1)} %all-gather.18.cloned.1.call-done, bf16[1024,1024]{1,0:T(8,128)(2,1)} %all-gather.16.cloned.1.call-done), kind=kOutput, calls=%fused_computation.75 | convolution fusion | flops 4322229248 | bytes 18882560 | tf_op jit(solution)/shard_map/dot_general | solution.py:135
  578.8 75.4 %reduce-scatter.13.cloned.1.call-done = bf16[512,1024]{1,0:T(8,128)(2,1)} async-done(((bf16[2048,1024]{1,0:T(8,128)(2,1)}), bf16[512,1024]{1,0:T(8,128)(2,1)}) %reduce-scatter.13.cloned.1.call-update) | async-done | bytes 1048592 | tf_op jit(solution)/shard_map/reduce_scatter | solution.py:149
  660.4 81.2 %all-gather.20.cloned.1.call-done = bf16[2048,1024]{1,0:T(8,128)(2,1)} async-done(((bf16[512,1024]{1,0:T(8,128)(2,1)}), bf16[2048,1024]{1,0:T(8,128)(2,1)}) %all-gather.20.cloned.1.call-update) | async-done | bytes 4194320 | tf_op jit(solution)/shard_map/all_gather | solution.py:164
  753.3 35.3 %while.27 = (s32[]{:T(128)}, bf16[4,512,4,64]{1,3,2,0:T(8,128)(2,1)S(1)}, bf16[4,512,4,64]{1,3,2,0:T(8,128)(2,1)}, bf16[4,512,4,64]{1,3,2,0:T(8,128)(2,1)}, bf16...) while((s32[]{:T(128)}, ...), condition=%wide.region_17.18_spmd, body=%wide.region_15.17_spmd.sunk | while | flops 687470592 | bytes 38338192 | solution.py:194
  811.7 8.4 fusion.85
  820.1 7.8 bitcast_convert_fusion
  828.0 10.6 fusion.96
  838.9 10.5 fusion.95
  857.4 41.9 %all-reduce = (f32[2,1024]{1,0:T(2,128)S(1)}, f32[1024]{0:T(1024)}, f32[1024]{0:T(1024)}, f32[1024]{0:T(1024)}, f32[4096]{0:T(1024)S(1)}, /*index=5*/f32[1024]{0:T(1024)}, f32[1024]{0:T(1024)}, f32[1024]{0:T(1024)}) all-reduce(f32[2,1024]{1,0:T(2,128)S(1)} %maximum_dynamic-update-slice_fusion,, ...), channel_id=1, replica_groups=mesh['dp'=8,'tensor'=4] {'dp','tensor'}, use_global_device_ids=true, to_apply=%region_22.23 | all-reduce | flops 12288 | bytes 98304 | tf_op jit(solution)/shard_map/psum | solution.py:239
  902.4 42.9 %reduce-scatter.15.cloned.1.call-done = bf16[512,1024]{1,0:T(8,128)(2,1)} async-done(((bf16[2048,1024]{1,0:T(8,128)(2,1)}), bf16[512,1024]{1,0:T(8,128)(2,1)}) %reduce-scatter.15.cloned.1.call-update) | async-done | bytes 1048592 | tf_op jit(solution)/shard_map/reduce_scatter | solution.py:216
  948.9 52.4 %reduce-scatter.23.cloned.1.call-done = f32[128,1024]{1,0:T(8,128)} async-done(((f32[1024,1024]{1,0:T(8,128)}), f32[128,1024]{1,0:T(8,128)}) %reduce-scatter.23.cloned.1.call-update) | async-done | bytes 524304 | tf_op jit(solution)/shard_map/reduce_scatter | solution.py:230
  1001.3 55.1 %reduce-scatter.21.cloned.1.call-done = f32[128,1024]{1,0:T(8,128)} async-done(((f32[1024,1024]{1,0:T(8,128)}), f32[128,1024]{1,0:T(8,128)}) %reduce-scatter.21.cloned.1.call-update) | async-done | bytes 524304 | tf_op jit(solution)/shard_map/reduce_scatter | solution.py:229
  1056.4 40.0 %reduce-scatter.19.cloned.1.call-done = f32[128,256]{1,0:T(8,128)} async-done(((f32[1024,256]{1,0:T(8,128)}), f32[128,256]{1,0:T(8,128)}) %reduce-scatter.19.cloned.1.call-update) | async-done | bytes 131088 | tf_op jit(solution)/shard_map/reduce_scatter | solution.py:228
  (207 shorter events, 165.9 us)
Async XLA Ops:
  7.2 31.2 %all-gather.10.cloned.1.call-start = ((), (), s32[]{:S(2)}) async-start(), calls=%async_computation.9 | async-start | bytes 1769472 | tf_op jit(solution)/shard_map/all_gather | solution.py:62
  7.9 112.8 %all-gather.8.cloned.1.call-start = ((), (), s32[]{:S(2)}) async-start(), calls=%async_computation.8 | async-start | bytes 5242880 | tf_op jit(solution)/shard_map/all_gather | solution.py:67
  8.7 234.4 %reduce-scatter.9.cloned.1.call-start = ((), (), s32[]{:S(2)}) async-start(), calls=%async_computation.10 | async-start | bytes 5242880 | tf_op jit(solution)/shard_map/reduce_scatter | solution.py:94
  167.6 75.5 %copy-start = (bf16[512,1024]{1,0:T(8,128)(2,1)S(1)}, bf16[512,1024]{1,0:T(8,128)(2,1)}, u32[]{:S(2)}) copy-start(bf16[512,1024]{1,0:T(8,128)(2,1)} %param.19) | copy-start | bytes 3145732
  167.6 105.8 %all-gather.14.cloned.1.call-start = ((), (), s32[]{:S(2)}) async-start(), calls=%async_computation.12 | async-start | bytes 2359296 | tf_op jit(solution)/shard_map/all_gather | solution.py:64
  168.2 188.1 %all-gather.12.cloned.1.call-start = ((), (), s32[]{:S(2)}) async-start(), calls=%async_computation.11 | async-start | bytes 5242880 | tf_op jit(solution)/shard_map/all_gather | solution.py:105
  168.5 80.3 %copy-start.15 = (bf16[1024]{0:T(1024)(128)(2,1)S(1)}, bf16[1024]{0:T(1024)(128)(2,1)}, u32[]{:S(2)}) copy-start(bf16[1024]{0:T(1024)(128)(2,1)} %param.28) | copy-start | bytes 6148
  243.1 3.5 copy-start.1
  248.2 136.4 %all-gather.16.cloned.1.call-start = ((), (), s32[]{:S(2)}) async-start(), calls=%async_computation.13 | async-start | bytes 2359296 | tf_op jit(solution)/shard_map/all_gather | solution.py:65
  248.8 222.2 %reduce-scatter.11.cloned.1.call-start = ((), (), s32[]{:S(2)}) async-start(), calls=%async_computation.14 | async-start | bytes 5242880 | tf_op jit(solution)/shard_map/reduce_scatter | solution.py:111
  394.0 165.0 %all-gather.18.cloned.1.call-start = ((), (), s32[]{:S(2)}) async-start(), calls=%async_computation.15 | async-start | bytes 5242880 | tf_op jit(solution)/shard_map/all_gather | solution.py:134
  471.0 2.7 copy-start.8
  477.6 176.5 %reduce-scatter.13.cloned.1.call-start = ((), (), s32[]{:S(2)}) async-start(), calls=%async_computation.16 | async-start | bytes 5242880 | tf_op jit(solution)/shard_map/reduce_scatter | solution.py:149
  559.1 13.3 %copy-start.19 = (bf16[1024,1024]{1,0:T(8,128)(2,1)S(1)}, bf16[1024,1024]{1,0:T(8,128)(2,1)}, u32[]{:S(2)}) copy-start(bf16[1024,1024]{1,0:T(8,128)(2,1)} %all-gather.14.cloned.1.call-done) | copy-start | bytes 6291460
  578.7 162.9 %all-gather.20.cloned.1.call-start = ((), (), s32[]{:S(2)}) async-start(), calls=%async_computation.17 | async-start | bytes 5242880 | tf_op jit(solution)/shard_map/all_gather | solution.py:164
  654.2 3.3 copy-start.4
  654.2 3.3 copy-start.10
  660.2 240.3 %reduce-scatter.17.cloned.1.call-start = ((), (), s32[]{:S(2)}) async-start(), calls=%async_computation.19 | async-start | bytes 3538944 | tf_op jit(solution)/shard_map/reduce_scatter | solution.py:227
  745.2 8.1 copy-start.3
  788.6 7.2 copy-start.9
  820.1 125.2 %reduce-scatter.15.cloned.1.call-start = ((), (), s32[]{:S(2)}) async-start(), calls=%async_computation.18 | async-start | bytes 5242880 | tf_op jit(solution)/shard_map/reduce_scatter | solution.py:216
  827.9 173.3 %reduce-scatter.23.cloned.1.call-start = ((), (), s32[]{:S(2)}) async-start(), calls=%async_computation.22 | async-start | bytes 4718592 | tf_op jit(solution)/shard_map/reduce_scatter | solution.py:230
  838.6 217.8 %reduce-scatter.21.cloned.1.call-start = ((), (), s32[]{:S(2)}) async-start(), calls=%async_computation.21 | async-start | bytes 4718592 | tf_op jit(solution)/shard_map/reduce_scatter | solution.py:229
  849.4 247.0 %reduce-scatter.19.cloned.1.call-start = ((), (), s32[]{:S(2)}) async-start(), calls=%async_computation.20 | async-start | bytes 1179648 | tf_op jit(solution)/shard_map/reduce_scatter | solution.py:228
  (15 other events, 17.0 us)
Sparse Core Ops, SparseCore 0:
  9.9 28.3 all-gather.9
  39.9 80.7 all-gather.7
  167.7 75.2 reduce-scatter.8
  245.0 28.3 all-gather.13
  275.4 80.7 all-gather.11
  358.1 26.4 all-gather.15
  394.2 76.7 reduce-scatter.10
  477.7 81.2 all-gather.17
  578.8 75.2 reduce-scatter.12
  660.3 81.2 all-gather.19
  820.2 44.9 reduce-scatter.16
  867.3 77.9 reduce-scatter.14
  949.6 51.6 reduce-scatter.22
  1005.1 51.2 reduce-scatter.20
  1060.3 36.0 reduce-scatter.18
where the time goes:
time: 1110 us; the launch traced here: 1100 us
  waiting for transfers between devices  789 us (71%)
  matrix products  148 us (13%)
  local copies, waits for them, and re-layouts  60.4 us (5%)
  blocking collectives  55.1 us (5%)
  other arithmetic  34.6 us (3%)
  between operations  14.8 us (1%)
    all_gather x1, waiting for transfers between devices, body(): lax.all_gather(hidden.astype(jnp.bfloat16), 'tensor', axis=0, tiled=True)  82.9 us
    all_gather x1, waiting for transfers between devices, body(): gathered = lax.all_gather(tokens, 'tensor', axis=0, tiled=True)  82.4 us
    all_gather x1, waiting for transfers between devices, body(): grad_ffn_all = lax.all_gather(grad_ffn, 'tensor', axis=0, tiled=True)  81.4 us
    all_gather x1, waiting for transfers between devices, body(): grad_attn_all = lax.all_gather(grad_attn, 'tensor', axis=0, tiled=True)  81.2 us
    reduce_scatter x1, waiting for transfers between devices, body(): lax.psum_scatter(lax.dot_general(rows, full_back, CONTRACT_LAST, preferre...  76.2 us
    reduce_scatter x1, waiting for transfers between devices, body(): lax.psum_scatter(lax.dot_general(rows, back_in, CONTRACT_LAST, preferred_...  75.4 us
    reduce_scatter x1, waiting for transfers between devices, body(): lax.psum_scatter(lax.dot_general(rows, full_out, CONTRACT_LAST, preferred...  74.6 us
    reduce_scatter x1, waiting for transfers between devices, body(): lax.psum_scatter(grad_w_in, 'dp', scatter_dimension=0, tiled=True)  55.1 us
  transfers between devices with their start and end apart: 15, of which 14 were waited for; matrix products, arithmetic and copies ran while one was open for 7% of the time, Pallas kernels for 0%

commit v1 on v0

v1 whole, which is shorter than its diff:
```python
import functools

import jax
import jax.numpy as jnp
from jax import lax
from jax.experimental import pallas as pl
from jax.experimental.pallas import tpu as pltpu
from jax.sharding import PartitionSpec as P

H = 16
EPS = 1e-05
MASKED = -1000000000.0
SQRT_HALF = 0.7071067811865476
INV_ROOT_TAU = 0.3989422804014327
ROWS_NT = (((1,), (1,)), ((), ()))
ROWS_TN = (((0,), (0,)), ((), ()))
ALL = ("tensor", "dp")


def dot(a, b):
    return jnp.dot(a, b, preferred_element_type=jnp.float32)


def dot_nt(a, b):
    return lax.dot_general(a, b, ROWS_NT, preferred_element_type=jnp.float32)


def dot_tn(a, b):
    return lax.dot_general(a, b, ROWS_TN, preferred_element_type=jnp.float32)


def normalize(values, gain, shift):
    centre = values - jnp.mean(values, axis=-1, keepdims=True)
    inverse = lax.rsqrt(jnp.mean(centre * centre, axis=-1, keepdims=True) + EPS)
    scaled = centre * inverse
    return (scaled * gain + shift, scaled, inverse)


def norm_back(grad_out, scaled, inverse, gain):
    grad_scaled = grad_out * gain
    inner = jnp.mean(grad_scaled, axis=-1, keepdims=True)
    along = jnp.mean(grad_scaled * scaled, axis=-1, keepdims=True)
    return inverse * (grad_scaled - inner - scaled * along)


def softmax_of(query, key, limit, scale):
    scores = dot_nt(query, key) * scale
    column = lax.broadcasted_iota(jnp.int32, scores.shape, 1)
    scores = jnp.where(column < limit, scores, MASKED)
    expo = jnp.exp(scores - jnp.max(scores, axis=-1, keepdims=True))
    return expo * (1.0 / jnp.sum(expo, axis=-1, keepdims=True))


def attend_kernel(width, head, seq_len, limit_ref, qkv_ref, out_ref):
    limit = limit_ref[pl.program_id(0)]
    for at in range(width // head):
        low = at * head
        query = qkv_ref[:, low : low + head]
        key = qkv_ref[:, width + low : width + low + head]
        value = qkv_ref[:, 2 * width + low : 2 * width + low + head]
        probs = softmax_of(query, key, limit, head**-0.5).astype(jnp.bfloat16)
        out_ref[:, low : low + head] = dot(probs, value).astype(jnp.bfloat16)


def attend_back_kernel(width, head, seq_len, limit_ref, qkv_ref, grad_ref, out_ref):
    limit = limit_ref[pl.program_id(0)]
    scale = head**-0.5
    for at in range(width // head):
        low = at * head
        query = qkv_ref[:, low : low + head]
        key = qkv_ref[:, width + low : width + low + head]
        value = qkv_ref[:, 2 * width + low : 2 * width + low + head]
        grad = grad_ref[:, low : low + head]
        probs = softmax_of(query, key, limit, scale)
        grad_probs = dot_nt(grad, value)
        inner = jnp.sum(grad_probs * probs, axis=-1, keepdims=True)
        grad_scores = (probs * (grad_probs - inner)).astype(jnp.bfloat16)
        out_ref[:, low : low + head] = (dot(grad_scores, key) * scale).astype(jnp.bfloat16)
        out_ref[:, width + low : width + low + head] = (dot_tn(grad_scores, query) * scale).astype(
            jnp.bfloat16
        )
        out_ref[:, 2 * width + low : 2 * width + low + head] = dot_tn(
            probs.astype(jnp.bfloat16), grad
        ).astype(jnp.bfloat16)


def attend(limits, qkv, seq_len, width, head):
    rows = qkv.shape[0]
    groups = qkv.shape[1] // (3 * width)
    return pl.pallas_call(
        functools.partial(attend_kernel, width, head, seq_len),
        grid_spec=pltpu.PrefetchScalarGridSpec(
            num_scalar_prefetch=1,
            grid=(rows // seq_len, groups),
            in_specs=[pl.BlockSpec((seq_len, 3 * width), lambda s, g, lim: (s, g))],
            out_specs=pl.BlockSpec((seq_len, width), lambda s, g, lim: (s, g)),
        ),
        out_shape=jax.ShapeDtypeStruct((rows, groups * width), jnp.bfloat16),
        cost_estimate=pl.CostEstimate(
            flops=16 * rows * seq_len * groups * width,
            bytes_accessed=8 * rows * groups * width,
            transcendentals=rows * seq_len * groups * width // head,
        ),
    )(limits, qkv)


def attend_back(limits, qkv, grad, seq_len, width, head):
    rows = qkv.shape[0]
    groups = qkv.shape[1] // (3 * width)
    return pl.pallas_call(
        functools.partial(attend_back_kernel, width, head, seq_len),
        grid_spec=pltpu.PrefetchScalarGridSpec(
            num_scalar_prefetch=1,
            grid=(rows // seq_len, groups),
            in_specs=[
                pl.BlockSpec((seq_len, 3 * width), lambda s, g, lim: (s, g)),
                pl.BlockSpec((seq_len, width), lambda s, g, lim: (s, g)),
            ],
            out_specs=pl.BlockSpec((seq_len, 3 * width), lambda s, g, lim: (s, g)),
        ),
        out_shape=jax.ShapeDtypeStruct(qkv.shape, jnp.bfloat16),
        cost_estimate=pl.CostEstimate(
            flops=40 * rows * seq_len * groups * width,
            bytes_accessed=14 * rows * groups * width,
            transcendentals=rows * seq_len * groups * width // head,
        ),
    )(limits, qkv, grad)


def gather(weight):
    return lax.all_gather(weight, ALL, axis=0, tiled=True)


def scatter(parts):
    owners = lax.axis_size("dp")
    split = [
        part.astype(jnp.bfloat16).reshape(owners, part.shape[0] // owners, part.shape[1])
        for part in parts
    ]
    stacked = jnp.stack(split, axis=1).reshape(-1, parts[0].shape[1])
    own = lax.psum_scatter(stacked, "dp", scatter_dimension=0, tiled=True)
    return lax.psum_scatter(own, "tensor", scatter_dimension=0, tiled=True).astype(jnp.float32)


def body(
    tokens,
    lengths,
    w_qkv,
    b_qv,
    w_out,
    b_out,
    gain_one,
    shift_one,
    w_in,
    b_in,
    w_back,
    b_back,
    gain_two,
    shift_two,
    cotangent,
):
    groups = lax.axis_size("tensor")
    slot = lax.axis_index("tensor")
    rows, width = tokens.shape
    seq_len = rows * groups // lengths.shape[0]
    own_seqs = rows // seq_len
    part = w_qkv.shape[2]
    hidden_part = w_in.shape[1]
    head = width // H
    limits = lax.dynamic_slice_in_dim(lengths, slot * own_seqs, own_seqs, 0)

    def split(full):
        return [full[g * width : (g + 1) * width] for g in range(groups)]

    full_qkv = split(gather(w_qkv.reshape(w_qkv.shape[0], 3 * part)))
    full_out = split(gather(w_out))
    full_in = split(gather(w_in))
    full_back = split(gather(w_back))
    bias_qv_all = lax.all_gather(b_qv, "tensor", axis=1, tiled=True).astype(jnp.float32)
    bias_in_all = lax.all_gather(b_in, "tensor", axis=0, tiled=True).astype(jnp.float32)

    qkv_parts = []
    for g in range(groups):
        bias = bias_qv_all[:, g * part : (g + 1) * part]
        bias = jnp.concatenate([bias[0], jnp.zeros((part,), jnp.float32), bias[1]])
        qkv_parts.append((dot(tokens, full_qkv[g]) + bias).astype(jnp.bfloat16))
    qkv = jnp.concatenate(qkv_parts, axis=1)
    attended = attend(limits, qkv, seq_len, part, head)

    attn = sum(
        dot_nt(attended[:, g * part : (g + 1) * part], full_out[g]) for g in range(groups)
    )
    residual_one = tokens.astype(jnp.float32) + attn + b_out.astype(jnp.float32)
    gain_a = gain_one.astype(jnp.float32)
    hidden, scaled_one, inverse_one = normalize(residual_one, gain_a, shift_one.astype(jnp.float32))
    hidden_b = hidden.astype(jnp.bfloat16)

    pre_act = []
    activated = []
    for g in range(groups):
        pre = dot(hidden_b, full_in[g]) + bias_in_all[g * hidden_part : (g + 1) * hidden_part]
        pre_act.append(pre)
        activated.append(jax.nn.gelu(pre, approximate=False).astype(jnp.bfloat16))
    ffn = sum(dot_nt(activated[g], full_back[g]) for g in range(groups))
    residual_two = hidden + ffn + b_back.astype(jnp.float32)
    gain_b = gain_two.astype(jnp.float32)
    output, scaled_two, inverse_two = normalize(residual_two, gain_b, shift_two.astype(jnp.float32))

    grad_out = cotangent.astype(jnp.float32)
    grad_gain_two = jnp.sum(grad_out * scaled_two, axis=0)
    grad_shift_two = jnp.sum(grad_out, axis=0)
    grad_res_two = norm_back(grad_out, scaled_two, inverse_two, gain_b)
    grad_ffn = grad_res_two.astype(jnp.bfloat16)
    grad_b_back = jnp.sum(grad_ffn.astype(jnp.float32), axis=0)
    owner_back = scatter([dot_tn(grad_ffn, activated[g]) for g in range(groups)])

    grad_pre = []
    for g in range(groups):
        pre = pre_act[g]
        slope = 0.5 * (1.0 + lax.erf(pre * SQRT_HALF)) + pre * INV_ROOT_TAU * jnp.exp(
            -0.5 * pre * pre
        )
        grad_pre.append((dot(grad_ffn, full_back[g]) * slope).astype(jnp.bfloat16))
    grad_b_in = jnp.concatenate([jnp.sum(one.astype(jnp.float32), axis=0) for one in grad_pre])
    owner_in = scatter([dot_tn(hidden_b, grad_pre[g]) for g in range(groups)])
    grad_hidden = grad_res_two + sum(dot_nt(grad_pre[g], full_in[g]) for g in range(groups))
    grad_gain_one = jnp.sum(grad_hidden * scaled_one, axis=0)
    grad_shift_one = jnp.sum(grad_hidden, axis=0)
    grad_res_one = norm_back(grad_hidden, scaled_one, inverse_one, gain_a)
    grad_attn = grad_res_one.astype(jnp.bfloat16)
    grad_b_out = jnp.sum(grad_attn.astype(jnp.float32), axis=0)
    owner_out = scatter(
        [dot_tn(grad_attn, attended[:, g * part : (g + 1) * part]) for g in range(groups)]
    )
    grad_mixed = jnp.concatenate(
        [dot(grad_attn, full_out[g]).astype(jnp.bfloat16) for g in range(groups)], axis=1
    )
    grad_qkv = attend_back(limits, qkv, grad_mixed, seq_len, part, head)
    grad_parts = [grad_qkv[:, g * 3 * part : (g + 1) * 3 * part] for g in range(groups)]
    owner_qkv = scatter([dot_tn(tokens, grad_parts[g]) for g in range(groups)])
    grad_tokens = grad_res_one + sum(dot_nt(grad_parts[g], full_qkv[g]) for g in range(groups))
    grad_sums = jnp.sum(grad_qkv.astype(jnp.float32), axis=0).reshape(groups, 3, part)
    grad_b_qv = jnp.stack([grad_sums[:, 0].reshape(width), grad_sums[:, 2].reshape(width)])

    summed = lax.psum(
        (
            grad_b_qv,
            grad_b_in,
            grad_b_out,
            grad_gain_one,
            grad_shift_one,
            grad_b_back,
            grad_gain_two,
            grad_shift_two,
        ),
        ("dp", "tensor"),
    )
    owner_b_qv = lax.dynamic_slice_in_dim(summed[0], slot * part, part, 1)
    owner_b_in = lax.dynamic_slice_in_dim(summed[1], slot * hidden_part, hidden_part, 0)
    return (
        output.astype(jnp.bfloat16),
        grad_tokens,
        owner_qkv.reshape(w_qkv.shape),
        owner_b_qv,
        owner_out,
        summed[2],
        summed[3],
        summed[4],
        owner_in,
        owner_b_in,
        owner_back,
        summed[5],
        summed[6],
        summed[7],
    )


def solution(mesh):
    in_specs = (
        P(("dp", "tensor"), None),
        P("dp"),
        P("dp", None, "tensor"),
        P(None, "tensor"),
        P("dp", "tensor"),
        P(),
        P(),
        P(),
        P("dp", "tensor"),
        P("tensor"),
        P("dp", "tensor"),
        P(),
        P(),
        P(),
        P(("dp", "tensor"), None),
    )
    out_specs = (
        P(("dp", "tensor"), None),
        P(("dp", "tensor"), None),
        P("dp", None, "tensor"),
        P(None, "tensor"),
        P("dp", "tensor"),
        P(),
        P(),
        P(),
        P("dp", "tensor"),
        P("tensor"),
        P("dp", "tensor"),
        P(),
        P(),
        P(),
    )
    return jax.shard_map(body, mesh=mesh, in_specs=in_specs, out_specs=out_specs, check_vma=False)
```

time: 1110 us -> 736 us (0.66)
  waiting for transfers between devices: 789 us -> 437 us
  matrix products: 148 us -> 104 us
  Pallas kernels: 0 us -> 37.9 us
  local copies, waits for them, and re-layouts: 60.4 us -> 37.6 us
    reduce_scatter x8, waiting for transfers between devices: 417 us -> 214 us  [the longest x4 170 us: scatter(): own = lax.psum_scatter(stacked, 'dp', scatter_dimension=0, tiled=True)]
    all_gather x7 -> x4, waiting for transfers between devices: 370 us -> 221 us  [gather(): return lax.all_gather(weight, ALL, axis=0, tiled=True)]
    dot_general x40 -> x48, matrix products: 148 us -> 104 us  [the longest x16 46.5 us: dot(): return jnp.dot(a, b, preferred_element_type=jnp.float32)]
    pallas_call x0 -> x2, Pallas kernels: none -> 37.9 us  [the longest x1 22.9 us: attend_back(): pl.pallas_call(functools.partial(attend_back_kernel, width, head, seq_len...]
    another operation x0 -> x5, other arithmetic: none -> 13.6 us  [the longest x4 13.6 us: scatter(): stacked = jnp.stack(split, axis=1).reshape(-1, parts[0].shape[1])]
    reduce_sum x9 -> x1, other arithmetic: 12.6 us -> 0.64 us  [body(): jnp.sum(grad_qkv.astype(jnp.float32), axis=0).reshape(groups, 3, part)]
    all_gather x1 -> x2, blocking collectives: 13.2 us -> 24.9 us  [the longest x1 12.8 us: body(): lax.all_gather(b_qv, 'tensor', axis=1, tiled=True).astype(jnp.float32)]
    another operation x13 -> x8, local copies, waits for them, and re-layouts: 23.4 us -> 26.2 us  [the longest x7 26.2 us: scatter(): stacked = jnp.stack(split, axis=1).reshape(-1, parts[0].shape[1])]
  transfers between devices with their start and end apart: 15 -> 12, of which waited for: 14 -> 9; matrix products, arithmetic and copies ran while one was open for 7% -> 16% of each run, Pallas kernels for 0% -> 5%
where the time goes in v1:
time: 736 us; the launch traced here: 732 us
  waiting for transfers between devices  437 us (59%)
  matrix products  104 us (14%)
  blocking collectives  65.8 us (9%)
  Pallas kernels  37.9 us (5%)
  local copies, waits for them, and re-layouts  37.6 us (5%)
  other arithmetic  32.8 us (4%)
  between operations  15.2 us (2%)
    all_gather x4, waiting for transfers between devices, gather(): return lax.all_gather(weight, ALL, axis=0, tiled=True)  221 us
    reduce_scatter x4, waiting for transfers between devices, scatter(): own = lax.psum_scatter(stacked, 'dp', scatter_dimension=0, tiled=True)  170 us
    dot_general x16, matrix products, dot(): return jnp.dot(a, b, preferred_element_type=jnp.float32)  46.5 us
    reduce_scatter x4, waiting for transfers between devices, scatter(): lax.psum_scatter(own, 'tensor', scatter_dimension=0, tiled=True)  44.1 us
    psum x1, blocking collectives, body(): lax.psum((grad_b_qv, grad_b_in, grad_b_out, grad_gain_one, grad_shift_one...  40.9 us
    dot_general x16, matrix products, dot_nt(): return lax.dot_general(a, b, ROWS_NT, preferred_element_type=jnp.float32)  32 us
    another operation x7, local copies, waits for them, and re-layouts, scatter(): stacked = jnp.stack(split, axis=1).reshape(-1, parts[0].shape[1])  26.2 us
    dot_general x16, matrix products, dot_tn(): return lax.dot_general(a, b, ROWS_TN, preferred_element_type=jnp.float32)  25.5 us
  transfers between devices with their start and end apart: 12, of which 9 were waited for; matrix products, arithmetic and copies ran while one was open for 16% of the time, Pallas kernels for 5%

profile of v1, /device:TPU:0, one launch (start us, length us, event | category | flops | bytes accessed | tf_op | source)
XLA Modules:
  0.0 731.5 jit_solution(6638098751676704470)
XLA Ops:
  16.4 12.8 %all_gather.19 = bf16[2,1024]{1,0:T(2,128)(2,1)S(1)} all-gather(bf16[2,256]{1,0:T(2,128)(2,1)} %param.18), channel_id=1, replica_groups=mesh['dp'=8,'tensor'=4] {'tensor'}, dimensions={1}, use_global_device_ids=true | all-gather | bytes 5120 | tf_op jit(solution)/shard_map/all_gather | solution.py:179
  29.3 12.1 %all_gather.22 = bf16[4096]{0:T(1024)(128)(2,1)S(1)} all-gather(bf16[1024]{0:T(1024)(128)(2,1)} %param.24), channel_id=1, replica_groups=mesh['dp'=8,'tensor'=4] {'tensor'}, dimensions={0}, use_global_device_ids=true | all-gather | bytes 10240 | tf_op jit(solution)/shard_map/all_gather | solution.py:180
  41.4 51.9 %all-gather.5.cloned.1.call-done = bf16[4096,768]{0,1:T(8,128)(2,1)} async-done(((bf16[128,768]{0,1:T(8,128)(2,1)}), bf16[4096,768]{0,1:T(8,128)(2,1)}) %all-gather.5.cloned.1.call-update) | async-done | bytes 6291472 | tf_op jit(solution)/shard_map/all_gather | solution.py:131
  102.9 15.0 %shard_map.254 = bf16[512,1024]{1,0:T(8,128)(2,1)} custom-call(s32[1]{0:T(128)} %dynamic_slice.9.limit_ref, bf16[512,3072]{1,0:T(8,128)(2,1)} %pad_maximum_fusion.3.qkv_ref), custom_call_target="tpu_custom_call" | custom-call | flops 4294967296 | bytes 4194304 | tf_op jit(solution)/shard_map/pallas_call | solution.py:90
  117.9 32.8 %all-gather.7.cloned.1.call-done = bf16[4096,256]{1,0:T(8,128)(2,1)} async-done(((bf16[128,256]{1,0:T(8,128)(2,1)}), bf16[4096,256]{1,0:T(8,128)(2,1)}) %all-gather.7.cloned.1.call-update) | async-done | bytes 2097168 | tf_op jit(solution)/shard_map/all_gather | solution.py:131
  156.3 73.7 %all-gather.9.cloned.1.call-done = bf16[4096,1024]{1,0:T(8,128)(2,1)} async-done(((bf16[128,1024]{1,0:T(8,128)(2,1)}), bf16[4096,1024]{1,0:T(8,128)(2,1)}) %all-gather.9.cloned.1.call-update) | async-done | bytes 8388624 | tf_op jit(solution)/shard_map/all_gather | solution.py:131
  230.0 8.0 %fusion.17 = (bf16[512,1024]{1,0:T(8,128)(2,1)}, f32[512,1024]{1,0:T(8,128)}) fusion(f32[1024]{0:T(1024)S(1)} %get-tuple-element.69, bf16[512,1024]{1,0:T(8,128)(2,1)S(1)} %fusion.67, bf16[4096,1024]{1,0:T(8,128)(2,1)} %all-gather.9.cloned.1.call-done), kind=kOutput, calls=%fused_computation.33 | convolution fusion | flops 1108344832 | bytes 6295552 | tf_op jit(solution)/shard_map/dot_general | solution.py:21
  238.0 8.6 %fusion.14 = (bf16[512,1024]{1,0:T(8,128)(2,1)}, f32[512,1024]{1,0:T(8,128)}) fusion(f32[1024]{0:T(1024)S(1)} %get-tuple-element.68, bf16[512,1024]{1,0:T(8,128)(2,1)S(1)} %fusion.67, bf16[4096,1024]{1,0:T(8,128)(2,1)} %all-gather.9.cloned.1.call-done), kind=kOutput, calls=%fused_computation.30 | convolution fusion | flops 1108344832 | bytes 6295552 | tf_op jit(solution)/shard_map/dot_general | solution.py:21
  246.6 62.2 %all-gather.11.cloned.1.call-done = bf16[4096,1024]{1,0:T(8,128)(2,1)} async-done(((bf16[128,1024]{1,0:T(8,128)(2,1)}), bf16[4096,1024]{1,0:T(8,128)(2,1)}) %all-gather.11.cloned.1.call-update) | async-done | bytes 8388624 | tf_op jit(solution)/shard_map/all_gather | solution.py:131
  315.2 6.1 fusion.11
  322.7 6.2 fusion.8
  360.4 22.9 %shard_map.255 = bf16[512,3072]{1,0:T(8,128)(2,1)} custom-call(s32[1]{0:T(128)} %dynamic_slice.9.limit_ref, bf16[512,3072]{1,0:T(8,128)(2,1)} %pad_maximum_fusion.3.qkv_ref, bf16[512,1024]{1,0:T(8,128)(2,1)} %pad_maximum_fusion.5.grad_ref), custom_call_target="tpu_custom_call" | custom-call | flops 10737418240 | bytes 7340032 | tf_op jit(solution)/shard_map/pallas_call | solution.py:110
  404.1 5.3 pad_maximum_fusion.2
  416.3 4.2 pad_maximum_fusion.1
  420.4 8.9 %copy.62 = bf16[8,4,128,1024]{3,2,1,0:T(8,128)(2,1)} copy(bf16[8,4,128,1024]{3,2,0,1:T(8,128)(2,1)} %pad_maximum_fusion.1) | data formatting | bytes 16777216 | tf_op jit(solution)/shard_map/stack | solution.py:140
  436.3 3.8 pad_maximum_fusion
  440.1 8.2 %copy.61 = bf16[8,4,128,1024]{3,2,1,0:T(8,128)(2,1)} copy(bf16[8,4,128,1024]{3,2,0,1:T(8,128)(2,1)} %pad_maximum_fusion) | data formatting | bytes 16777216 | tf_op jit(solution)/shard_map/stack | solution.py:140
  449.1 20.9 %reduce-scatter.9.cloned.1.call-done = bf16[512,768]{1,0:T(8,128)(2,1)} async-done(((bf16[4096,768]{1,0:T(8,128)(2,1)}), bf16[512,768]{1,0:T(8,128)(2,1)}) %reduce-scatter.9.cloned.1.call-update) | async-done | bytes 786448 | tf_op jit(solution)/shard_map/reduce_scatter | solution.py:141
  470.1 74.7 %reduce-scatter.21.cloned.1.call-done = bf16[512,1024]{1,0:T(8,128)(2,1)} async-done(((bf16[4096,1024]{1,0:T(8,128)(2,1)}), bf16[512,1024]{1,0:T(8,128)(2,1)}) %reduce-scatter.21.cloned.1.call-update) | async-done | bytes 1048592 | tf_op jit(solution)/shard_map/reduce_scatter | solution.py:141
  545.7 74.3 %reduce-scatter.17.cloned.1.call-done = bf16[512,1024]{1,0:T(8,128)(2,1)} async-done(((bf16[4096,1024]{1,0:T(8,128)(2,1)}), bf16[512,1024]{1,0:T(8,128)(2,1)}) %reduce-scatter.17.cloned.1.call-update) | async-done | bytes 1048592 | tf_op jit(solution)/shard_map/reduce_scatter | solution.py:141
  620.1 40.9 %all-reduce = (f32[2,1024]{1,0:T(2,128)S(1)}, f32[1024]{0:T(1024)}, f32[1024]{0:T(1024)}, f32[1024]{0:T(1024)}, f32[4096]{0:T(1024)S(1)}, /*index=5*/f32[1024]{0:T(1024)}, f32[1024]{0:T(1024)}, f32[1024]{0:T(1024)}) all-reduce(f32[2,1024]{1,0:T(2,128)S(1)} %pad_maximum_fusion.11, ...), channel_id=1, replica_groups=mesh['dp'=8,'tensor'=4] {'dp','tensor'}, use_global_device_ids=true, to_apply=%region_11.0 | all-reduce | flops 12288 | bytes 98304 | tf_op jit(solution)/shard_map/psum | solution.py:245
  669.5 3.9 add_add_fusion
  676.8 17.9 %reduce-scatter.23.cloned.1.call-done = bf16[128,1024]{1,0:T(8,128)(2,1)} async-done(((bf16[512,1024]{1,0:T(8,128)(2,1)}), bf16[128,1024]{1,0:T(8,128)(2,1)}) %reduce-scatter.23.cloned.1.call-update) | async-done | bytes 262160 | tf_op jit(solution)/shard_map/reduce_scatter | solution.py:142
  696.6 26.2 %reduce-scatter.19.cloned.1.call-done = bf16[128,1024]{1,0:T(8,128)(2,1)} async-done(((bf16[512,1024]{1,0:T(8,128)(2,1)}), bf16[128,1024]{1,0:T(8,128)(2,1)}) %reduce-scatter.19.cloned.1.call-update) | async-done | bytes 262160 | tf_op jit(solution)/shard_map/reduce_scatter | solution.py:142
  (187 shorter events, 114.8 us)
Async XLA Ops:
  7.2 86.1 %all-gather.5.cloned.1.call-start = ((), (), s32[]{:S(2)}) async-start(), calls=%async_computation.8 | async-start | bytes 6488064 | tf_op jit(solution)/shard_map/all_gather | solution.py:131
  9.0 141.8 %all-gather.7.cloned.1.call-start = ((), (), s32[]{:S(2)}) async-start(), calls=%async_computation.9 | async-start | bytes 2162688 | tf_op jit(solution)/shard_map/all_gather | solution.py:131
  9.7 220.2 %all-gather.9.cloned.1.call-start = ((), (), s32[]{:S(2)}) async-start(), calls=%async_computation.10 | async-start | bytes 8650752 | tf_op jit(solution)/shard_map/all_gather | solution.py:131
  10.5 298.3 %all-gather.11.cloned.1.call-start = ((), (), s32[]{:S(2)}) async-start(), calls=%async_computation.11 | async-start | bytes 8650752 | tf_op jit(solution)/shard_map/all_gather | solution.py:131
  11.1 437.4 %reduce-scatter.13.cloned.1.call-start = ((), (), s32[]{:S(2)}) async-start(), calls=%async_computation.14 | async-start | bytes 2359296 | tf_op jit(solution)/shard_map/reduce_scatter | solution.py:141
  93.3 5.4 copy-start.15
  156.3 166.4 %copy-start.7 = (bf16[512,1024]{1,0:T(8,128)(2,1)}, bf16[512,1024]{1,0:T(8,128)(2,1)S(1)}, u32[]{:S(2)}) copy-start(bf16[512,1024]{1,0:T(8,128)(2,1)S(1)} %fusion.67) | copy-start | bytes 3145732
  308.8 6.4 slice-start
  312.1 9.2 %slice-start.2 = ((s8[8388608]{0:T(1024)(128)(4,1)}), s8[4194304]{0:T(1024)(128)(4,1)S(1)}, s32[]{:S(2)}) async-start(s8[8388608]{0:T(1024)(128)(4,1)} %bitcast.122), calls=%async_computation.22 | async-start | bytes 8388608
  315.2 6.2 slice-start.3
  334.9 6.5 copy-start.9
  337.0 6.5 copy-start.23
  339.1 5.7 copy-start.25
  341.4 4.7 copy-start.27
  343.5 3.9 copy-start.5
  356.0 114.1 %reduce-scatter.9.cloned.1.call-start = ((), (), s32[]{:S(2)}) async-start(), calls=%async_computation.12 | async-start | bytes 7077888 | tf_op jit(solution)/shard_map/reduce_scatter | solution.py:141
  360.4 22.9 %copy-start.12 = (bf16[512,1024]{1,0:T(8,128)(2,1)S(1)}, bf16[512,1024]{1,0:T(8,128)(2,1)}, u32[]{:S(2)}) copy-start(bf16[512,1024]{1,0:T(8,128)(2,1)} %param.15) | copy-start | bytes 3145732
  409.5 135.3 %reduce-scatter.21.cloned.1.call-start = ((), (), s32[]{:S(2)}) async-start(), calls=%async_computation.18 | async-start | bytes 9437184 | tf_op jit(solution)/shard_map/reduce_scatter | solution.py:141
  429.4 190.6 %reduce-scatter.17.cloned.1.call-start = ((), (), s32[]{:S(2)}) async-start(), calls=%async_computation.16 | async-start | bytes 9437184 | tf_op jit(solution)/shard_map/reduce_scatter | solution.py:141
  448.3 96.7 %copy-start.2 = (bf16[512,3072]{1,0:T(8,128)(2,1)S(1)}, bf16[512,3072]{1,0:T(8,128)(2,1)}, u32[]{:S(2)}) copy-start(bf16[512,3072]{1,0:T(8,128)(2,1)} %shard_map.255) | copy-start | bytes 9437188
  448.4 225.0 %reduce-scatter.15.cloned.1.call-start = ((), (), s32[]{:S(2)}) async-start(), calls=%async_computation.15 | async-start | bytes 327680 | tf_op jit(solution)/shard_map/reduce_scatter | solution.py:142
  449.1 225.8 %reduce-scatter.11.cloned.1.call-start = ((), (), s32[]{:S(2)}) async-start(), calls=%async_computation.13 | async-start | bytes 983040 | tf_op jit(solution)/shard_map/reduce_scatter | solution.py:142
  470.1 224.7 %reduce-scatter.23.cloned.1.call-start = ((), (), s32[]{:S(2)}) async-start(), calls=%async_computation.19 | async-start | bytes 1310720 | tf_op jit(solution)/shard_map/reduce_scatter | solution.py:142
  544.8 177.9 %reduce-scatter.19.cloned.1.call-start = ((), (), s32[]{:S(2)}) async-start(), calls=%async_computation.17 | async-start | bytes 1310720 | tf_op jit(solution)/shard_map/reduce_scatter | solution.py:142
  (23 other events, 43.8 us)
Sparse Core Ops, SparseCore 0:
  11.4 81.8 all-gather.4
  96.2 54.5 all-gather.6
  153.6 76.2 all-gather.8
  232.7 76.0 all-gather.10
  356.1 39.8 reduce-scatter.12
  409.6 60.3 reduce-scatter.8
  473.5 71.2 reduce-scatter.20
  548.7 71.2 reduce-scatter.16
  622.3 19.6 reduce-scatter.14
  644.2 21.7 reduce-scatter.10
  668.4 26.3 reduce-scatter.22
  696.9 25.7 reduce-scatter.18

commit v2 on v1

--- a/solution.py
+++ b/solution.py
@@ -14,7 +14,6 @@
 INV_ROOT_TAU = 0.3989422804014327
 ROWS_NT = (((1,), (1,)), ((), ()))
 ROWS_TN = (((0,), (0,)), ((), ()))
-ALL = ("tensor", "dp")
 
 
 def dot(a, b):
@@ -127,19 +126,101 @@
     )(limits, qkv, grad)
 
 
+def bit_orders():
+    bits = lax.axis_size("dp").bit_length() - 1
+    outer = list(range(1, bits))
+    return outer, outer[::-1]
+
+
+def exchange(value, bit):
+    size = lax.axis_size("dp")
+    return lax.ppermute(value, "dp", [(i, i ^ (1 << bit)) for i in range(size)])
+
+
+def rank(bit):
+    return lax.axis_size("dp") if bit == 0 else bit
+
+
 def gather(weight):
-    return lax.all_gather(weight, ALL, axis=0, tiled=True)
+    stacked = lax.all_gather(weight, "tensor", axis=0)
+    groups, rows, columns = stacked.shape
+    result = []
+    for g in range(groups):
+        order = bit_orders()[0 if 2 * g < groups else 1] + [0]
+        held, seen = stacked[g], []
+        for bit in order:
+            other = exchange(held, bit)
+            before = 2 ** sum(1 for one in seen if rank(one) > rank(bit))
+            shape = (before, held.shape[0] // before, columns)
+            held = jnp.stack([held.reshape(shape), other.reshape(shape)], axis=1)
+            held = held.reshape(-1, columns)
+            seen.append(bit)
+        result.append(held)
+    return result
 
 
 def scatter(parts):
-    owners = lax.axis_size("dp")
-    split = [
-        part.astype(jnp.bfloat16).reshape(owners, part.shape[0] // owners, part.shape[1])
-        for part in parts
-    ]
-    stacked = jnp.stack(split, axis=1).reshape(-1, parts[0].shape[1])
-    own = lax.psum_scatter(stacked, "dp", scatter_dimension=0, tiled=True)
-    return lax.psum_scatter(own, "tensor", scatter_dimension=0, tiled=True).astype(jnp.float32)
+    groups = len(parts)
+    owned = []
+    for g in range(groups):
+        order = [0] + bit_orders()[0 if 2 * g < groups else 1][::-1]
+        held = parts[g].astype(jnp.bfloat16)
+        columns = held.shape[1]
+        left = list(order)
+        for bit in order:
+            before = 2 ** sum(1 for one in left if rank(one) > rank(bit))
+            view = held.reshape(before, 2, -1, columns)
+            other = exchange(view[:, 1].reshape(-1, columns), bit)
+            held = view[:, 0].reshape(-1, columns) + other
+            left.remove(bit)
+        owned.append(held)
+    stacked = jnp.concatenate(owned, axis=0)
+    return lax.psum_scatter(stacked, "tensor", scatter_dimension=0, tiled=True).astype(jnp.float32)
+
+
+def block_sources():
+    size = lax.axis_size("dp")
+    bits = size.bit_length() - 1
+    major = sorted(range(bits), key=rank, reverse=True)
+    places = []
+    for at in range(size):
+        place = 0
+        for depth, bit in enumerate(major):
+            if (at >> (bits - 1 - depth)) & 1:
+                place += 1 << bit
+        places.append(place)
+    return places
+
+
+def to_own_order(value):
+    me = lax.axis_index("dp")
+    places = block_sources()
+    axis = value.ndim - 1
+    block = value.shape[axis] // len(places)
+    return jnp.concatenate(
+        [
+            lax.dynamic_slice_in_dim(value, jnp.bitwise_xor(me, place) * block, block, axis)
+            for place in places
+        ],
+        axis=axis,
+    )
+
+
+def from_own_order(value):
+    me = lax.axis_index("dp")
+    places = block_sources()
+    slot_of = jnp.array([places.index(i) for i in range(len(places))], jnp.int32)
+    axis = value.ndim - 1
+    block = value.shape[axis] // len(places)
+    return jnp.concatenate(
+        [
+            lax.dynamic_slice_in_dim(
+                value, slot_of[jnp.bitwise_xor(me, i)] * block, block, axis
+            )
+            for i in range(len(places))
+        ],
+        axis=axis,
+    )
 
 
 def body(
@@ -169,13 +250,17 @@
     head = width // H
     limits = lax.dynamic_slice_in_dim(lengths, slot * own_seqs, own_seqs, 0)
 
-    def split(full):
-        return [full[g * width : (g + 1) * width] for g in range(groups)]
-
-    full_qkv = split(gather(w_qkv.reshape(w_qkv.shape[0], 3 * part)))
-    full_out = split(gather(w_out))
-    full_in = split(gather(w_in))
-    full_back = split(gather(w_back))
+    first = gather(jnp.concatenate([w_qkv.reshape(w_qkv.shape[0], 3 * part), w_out], axis=1))
+    full_qkv = [one[:, : 3 * part] for one in first]
+    full_out = [one[:, 3 * part :] for one in first]
+    full_in = gather(w_in)
+    full_back = gather(w_back)
+    tokens = to_own_order(tokens)
+    cotangent = to_own_order(cotangent)
+    vectors = to_own_order(
+        jnp.stack([b_out, gain_one, shift_one, b_back, gain_two, shift_two]).astype(jnp.float32)
+    )
+    b_out, gain_one, shift_one, b_back, gain_two, shift_two = [vectors[i] for i in range(6)]
     bias_qv_all = lax.all_gather(b_qv, "tensor", axis=1, tiled=True).astype(jnp.float32)
     bias_in_all = lax.all_gather(b_in, "tensor", axis=0, tiled=True).astype(jnp.float32)
 
@@ -242,24 +327,28 @@
     grad_sums = jnp.sum(grad_qkv.astype(jnp.float32), axis=0).reshape(groups, 3, part)
     grad_b_qv = jnp.stack([grad_sums[:, 0].reshape(width), grad_sums[:, 2].reshape(width)])
 
-    summed = lax.psum(
-        (
-            grad_b_qv,
-            grad_b_in,
-            grad_b_out,
-            grad_gain_one,
-            grad_shift_one,
-            grad_b_back,
-            grad_gain_two,
-            grad_shift_two,
-        ),
+    early = from_own_order(
+        jnp.stack(
+            [
+                grad_b_out,
+                grad_gain_one,
+                grad_shift_one,
+                grad_b_back,
+                grad_gain_two,
+                grad_shift_two,
+            ]
+        )
+    )
+    early, late = lax.psum(
+        (jnp.concatenate([early, grad_b_in.reshape(-1, width)], axis=0), grad_b_qv),
         ("dp", "tensor"),
     )
+    summed = [late, early[6:].reshape(-1)] + [early[i] for i in range(6)]
     owner_b_qv = lax.dynamic_slice_in_dim(summed[0], slot * part, part, 1)
     owner_b_in = lax.dynamic_slice_in_dim(summed[1], slot * hidden_part, hidden_part, 0)
     return (
-        output.astype(jnp.bfloat16),
-        grad_tokens,
+        from_own_order(output.astype(jnp.bfloat16)),
+        from_own_order(grad_tokens),
         owner_qkv.reshape(w_qkv.shape),
         owner_b_qv,
         owner_out,

time: 736 us -> 688 us (0.935)
  waiting for transfers between devices: 437 us -> 201 us
  starting transfers between devices: 1.05 us -> 78.9 us
  other arithmetic: 32.8 us -> 88.5 us
  local copies, waits for them, and re-layouts: 37.6 us -> 79.1 us
    all_gather x4 -> x3, waiting for transfers between devices: 221 us -> 33.9 us  [gather(): stacked = lax.all_gather(weight, 'tensor', axis=0)]
    reduce_scatter x8 -> x4, waiting for transfers between devices: 214 us -> 30.6 us  [scatter(): lax.psum_scatter(stacked, 'tensor', scatter_dimension=0, tiled=True)]
    ppermute x0 -> x84, waiting for transfers between devices: none -> 135 us  [exchange(): return lax.ppermute(value, 'dp', [(i, i ^ 1 << bit) for i in range(size)])]
    ppermute x0 -> x84, starting transfers between devices: none -> 78.3 us  [exchange(): return lax.ppermute(value, 'dp', [(i, i ^ 1 << bit) for i in range(size)])]
    another operation x4 -> x36, other arithmetic: 13.6 us -> 54.7 us  [gather(): held = jnp.stack([held.reshape(shape), other.reshape(shape)], axis=1)]
    another operation x8 -> x62, local copies, waits for them, and re-layouts: 26.2 us -> 44.4 us  [the longest x40 21.7 us: scatter(): other = exchange(view[:, 1].reshape(-1, columns), bit)]
    unnamed x72 -> x270, local copies, waits for them, and re-layouts: 7.85 us -> 24.8 us
    add x0 -> x48, other arithmetic: none -> 16.6 us  [scatter(): held = view[:, 0].reshape(-1, columns) + other]
  transfers between devices with their start and end apart: 12 -> 91, of which waited for: 9 -> 32; matrix products, arithmetic and copies ran while one was open for 16% -> 23% of each run, Pallas kernels for 5% -> 2%
where the time goes in v2:
time: 688 us; the launch traced here: 680 us
  waiting for transfers between devices  201 us (29%)
  matrix products  107 us (16%)
  other arithmetic  88.5 us (13%)
  local copies, waits for them, and re-layouts  79.1 us (11%)
  starting transfers between devices  78.9 us (11%)
  blocking collectives  65 us (9%)
  Pallas kernels  38 us (6%)
  between operations  22.1 us (3%)
    ppermute x84, waiting for transfers between devices, exchange(): return lax.ppermute(value, 'dp', [(i, i ^ 1 << bit) for i in range(size)])  135 us
    ppermute x84, starting transfers between devices, exchange(): return lax.ppermute(value, 'dp', [(i, i ^ 1 << bit) for i in range(size)])  78.3 us
    another operation x36, other arithmetic, gather(): held = jnp.stack([held.reshape(shape), other.reshape(shape)], axis=1)  54.7 us
    dot_general x16, matrix products, dot(): return jnp.dot(a, b, preferred_element_type=jnp.float32)  42.8 us
    psum x1, blocking collectives, body(): lax.psum((jnp.concatenate([early, grad_b_in.reshape(-1, width)], axis=0),...  40.2 us
    dot_general x16, matrix products, dot_tn(): return lax.dot_general(a, b, ROWS_TN, preferred_element_type=jnp.float32)  35.3 us
    all_gather x3, waiting for transfers between devices, gather(): stacked = lax.all_gather(weight, 'tensor', axis=0)  33.9 us
    reduce_scatter x4, waiting for transfers between devices, scatter(): lax.psum_scatter(stacked, 'tensor', scatter_dimension=0, tiled=True)  30.6 us
  transfers between devices with their start and end apart: 91, of which 32 were waited for; matrix products, arithmetic and copies ran while one was open for 23% of the time, Pallas kernels for 2%

profile of v2, /device:TPU:0, one launch (start us, length us, event | category | flops | bytes accessed | tf_op | source)
XLA Modules:
  0.0 679.6 jit_solution(12276834143746244388)
XLA Ops:
  11.7 13.0 %all_gather.26 = bf16[2,1024]{1,0:T(2,128)(2,1)S(1)} all-gather(bf16[2,256]{1,0:T(2,128)(2,1)} %param.21), channel_id=1, replica_groups=mesh['dp'=8,'tensor'=4] {'tensor'}, dimensions={1}, use_global_device_ids=true | all-gather | bytes 5120 | tf_op jit(solution)/shard_map/all_gather | solution.py:264
  41.6 11.9 %all_gather.29 = bf16[4096]{0:T(1024)(128)(2,1)S(1)} all-gather(bf16[1024]{0:T(1024)(128)(2,1)S(1)} %copy-done.92), channel_id=1, replica_groups=mesh['dp'=8,'tensor'=4] {'tensor'}, dimensions={0}, use_global_device_ids=true | all-gather | bytes 10240 | tf_op jit(solution)/shard_map/all_gather | solution.py:265
  62.2 8.8 %all-gather.11.cloned.1.call-done = bf16[512,1024]{1,0:T(8,128)(2,1)} async-done(((bf16[128,1024]{1,0:T(8,128)(2,1)}), bf16[512,1024]{1,0:T(8,128)(2,1)}) %all-gather.11.cloned.1.call-update) | async-done | bytes 1048592 | tf_op jit(solution)/shard_map/all_gather | solution.py:145
  75.0 25.1 %all-gather.9.cloned.1.call-done = bf16[512,1024]{1,0:T(8,128)(2,1)} async-done(((bf16[128,1024]{1,0:T(8,128)(2,1)}), bf16[512,1024]{1,0:T(8,128)(2,1)}) %all-gather.9.cloned.1.call-update) | async-done | bytes 1048592 | tf_op jit(solution)/shard_map/all_gather | solution.py:145
  140.2 14.7 %collective-permute-done.12 = bf16[128,1024]{1,0:T(8,128)(2,1)S(1)} collective-permute-done((bf16[128,1024]{1,0:T(8,128)(2,1)}, bf16[128,1024]{1,0:T(8,128)(2,1)S(1)}, u32[]{:S(2)}, u32[]{:S(2)}) %collective-permute-start.12) | collective-permute-done | bytes 262176 | tf_op jit(solution)/shard_map/ppermute | solution.py:137
  174.5 6.9 %collective-permute-done.13 = bf16[256,1024]{1,0:T(8,128)(2,1)} collective-permute-done((bf16[256,1024]{1,0:T(8,128)(2,1)}, bf16[256,1024]{1,0:T(8,128)(2,1)}, u32[]{:S(2)}, u32[]{:S(2)}) %collective-permute-start.13) | collective-permute-done | bytes 524320 | tf_op jit(solution)/shard_map/ppermute | solution.py:137
  186.7 4.1 collective-permute-done.31
  234.4 15.4 %shard_map.281 = bf16[512,1024]{1,0:T(8,128)(2,1)} custom-call(s32[1]{0:T(128)} %dynamic_slice.233.limit_ref, bf16[512,3072]{1,0:T(8,128)(2,1)} %pad_maximum_fusion.qkv_ref), custom_call_target="tpu_custom_call" | custom-call | flops 4294967296 | bytes 4194304 | tf_op jit(solution)/shard_map/pallas_call | solution.py:89
  262.7 6.7 fusion.17
  269.4 6.6 fusion.11
  278.0 6.8 %fusion.8 = (bf16[512,1024]{1,0:T(8,128)(2,1)S(1)}, f32[512,1024]{1,0:T(8,128)}) fusion(f32[1024]{0:T(1024)S(1)} %get-tuple-element.140, bf16[512,1024]{1,0:T(8,128)(2,1)S(1)} %fusion.67, bf16[1024,1024]{1,0:T(8,128)(2,1)S(1)} %bitcast.637), kind=kOutput, calls=%fused_computation.21 | convolution fusion | flops 1108344832 | bytes 6295552 | tf_op jit(solution)/shard_map/dot_general | solution.py:20
  286.9 6.6 fusion.14
  320.4 22.7 %shard_map.282 = bf16[512,3072]{1,0:T(8,128)(2,1)} custom-call(s32[1]{0:T(128)} %dynamic_slice.233.limit_ref, bf16[512,3072]{1,0:T(8,128)(2,1)} %pad_maximum_fusion.qkv_ref, bf16[512,1024]{1,0:T(8,128)(2,1)} %pad_maximum_fusion.25.grad_ref), custom_call_target="tpu_custom_call" | custom-call | flops 10737418240 | bytes 7340032 | tf_op jit(solution)/shard_map/pallas_call | solution.py:109
  343.1 4.2 fusion.70
  388.2 40.2 %all-reduce = (f32[2,1024]{1,0:T(2,128)S(1)}, f32[10,1024]{1,0:T(8,128)S(1)}) all-reduce(f32[2,1024]{1,0:T(2,128)S(1)} %pad_maximum_fusion.49, f32[10,1024]{1,0:T(8,128)S(1)} %pad_maximum_fusion.43), channel_id=1, replica_groups=mesh['dp'=8,'tensor'=4] {'dp','tensor'}, use_global_device_ids=true, to_apply=%region_10.0 | all-reduce | flops 12288 | bytes 98304 | tf_op jit(solution)/shard_map/psum | solution.py:342
  467.9 4.1 collective-permute-done.52
  516.5 6.8 collective-permute-done.40
  529.9 24.3 %collective-permute-done.38 = bf16[128,768]{1,0:T(8,128)(2,1)S(1)} collective-permute-done((bf16[128,768]{1,0:T(8,128)(2,1)S(1)}, bf16[128,768]{1,0:T(8,128)(2,1)S(1)}, u32[]{:S(2)}, u32[]{:S(2)}) %collective-permute-start.38) | collective-permute-done | bytes 196640 | tf_op jit(solution)/shard_map/ppermute | solution.py:137
  555.7 4.7 collective-permute-done.41
  560.8 5.3 collective-permute-done.47
  566.6 6.1 collective-permute-done.44
  592.9 12.8 %collective-permute-done.74 = bf16[128,1024]{1,0:T(8,128)(2,1)S(1)} collective-permute-done((bf16[128,1024]{1,0:T(8,128)(2,1)S(1)}, bf16[128,1024]{1,0:T(8,128)(2,1)S(1)}, u32[]{:S(2)}, u32[]{:S(2)}) %collective-permute-start.74) | collective-permute-done | bytes 262176 | tf_op jit(solution)/shard_map/ppermute | solution.py:137
  638.1 4.2 reduce-scatter.11.cloned.1.call-done
  644.1 26.3 %reduce-scatter.9.cloned.1.call-done = bf16[128,1024]{1,0:T(8,128)(2,1)} async-done(((bf16[512,1024]{1,0:T(8,128)(2,1)}), bf16[128,1024]{1,0:T(8,128)(2,1)}) %reduce-scatter.9.cloned.1.call-update) | async-done | bytes 262160 | tf_op jit(solution)/shard_map/reduce_scatter | solution.py:178
  (690 shorter events, 369.3 us)
Async XLA Ops:
  7.2 48.6 %all-gather.7.cloned.1.call-start = ((), (), s32[]{:S(2)}) async-start(), calls=%async_computation.8 | async-start | bytes 1310720 | tf_op jit(solution)/shard_map/all_gather | solution.py:145
  10.1 60.9 %all-gather.11.cloned.1.call-start = ((), (), s32[]{:S(2)}) async-start(), calls=%async_computation.10 | async-start | bytes 1310720 | tf_op jit(solution)/shard_map/all_gather | solution.py:145
  10.9 89.2 %all-gather.9.cloned.1.call-start = ((), (), s32[]{:S(2)}) async-start(), calls=%async_computation.9 | async-start | bytes 1310720 | tf_op jit(solution)/shard_map/all_gather | solution.py:145
  11.6 623.0 %reduce-scatter.7.cloned.1.call-start = ((), (), s32[]{:S(2)}) async-start(), calls=%async_computation.5 | async-start | bytes 327680 | tf_op jit(solution)/shard_map/reduce_scatter | solution.py:178
  58.2 47.6 %collective-permute-start.6 = (bf16[128,1024]{0,1:T(8,128)(2,1)S(1)}, bf16[128,1024]{0,1:T(8,128)(2,1)}, u32[]{:S(2)}, u32[]{:S(2)}) collective-permute-start(bf16[128,1024]{0,1:T(8,128)(2,1)S(1)} %get-tuple-element.100), channel_id=1, source_target_pairs={{0,16},{4,20},{8,24},{12,28},{16,0},{20,4},{24,8},{28,12},{1,17},{... | collective-permute-start | bytes 786440 | tf_op jit(solution)/shard_map/ppermute | solution.py:137
  59.7 65.0 %collective-permute-start.3 = (bf16[128,1024]{0,1:T(8,128)(2,1)}, bf16[128,1024]{0,1:T(8,128)(2,1)}, u32[]{:S(2)}, u32[]{:S(2)}) collective-permute-start(bf16[128,1024]{0,1:T(8,128)(2,1)} %get-tuple-element.101), channel_id=1, source_target_pairs={{0,8},{4,12},{8,0},{12,4},{16,24},{20,28},{24,16},{28,20},{1,9},{5... | collective-permute-start | bytes 786440 | tf_op jit(solution)/shard_map/ppermute | solution.py:137
  61.2 59.1 %collective-permute-start = (bf16[128,1024]{0,1:T(8,128)(2,1)}, bf16[128,1024]{0,1:T(8,128)(2,1)}, u32[]{:S(2)}, u32[]{:S(2)}) collective-permute-start(bf16[128,1024]{0,1:T(8,128)(2,1)} %get-tuple-element.102), channel_id=1, source_target_pairs={{0,8},{4,12},{8,0},{12,4},{16,24},{20,28},{24,16},{28,20},{1,9},{5... | collective-permute-start | bytes 786440 | tf_op jit(solution)/shard_map/ppermute | solution.py:137
  61.7 40.7 %collective-permute-start.9 = (bf16[128,1024]{0,1:T(8,128)(2,1)}, bf16[128,1024]{0,1:T(8,128)(2,1)}, u32[]{:S(2)}, u32[]{:S(2)}) collective-permute-start(bf16[128,1024]{0,1:T(8,128)(2,1)} %get-tuple-element.103), channel_id=1, source_target_pairs={{0,16},{4,20},{8,24},{12,28},{16,0},{20,4},{24,8},{28,12},{1,17},{... | collective-permute-start | bytes 786440 | tf_op jit(solution)/shard_map/ppermute | solution.py:137
  73.5 39.6 %collective-permute-start.27 = (bf16[128,1024]{1,0:T(8,128)(2,1)}, bf16[128,1024]{1,0:T(8,128)(2,1)}, u32[]{:S(2)}, u32[]{:S(2)}) collective-permute-start(bf16[128,1024]{1,0:T(8,128)(2,1)} %get-tuple-element.84), channel_id=1, source_target_pairs={{0,16},{4,20},{8,24},{12,28},{16,0},{20,4},{24,8},{28,12},{1,17},{... | collective-permute-start | bytes 786440 | tf_op jit(solution)/shard_map/ppermute | solution.py:137
  126.4 32.5 %collective-permute-start.10 = (bf16[256,1024]{1,0:T(8,128)(2,1)}, bf16[256,1024]{1,0:T(8,128)(2,1)}, u32[]{:S(2)}, u32[]{:S(2)}) collective-permute-start(bf16[256,1024]{1,0:T(8,128)(2,1)} %bitcast.697), channel_id=1, source_target_pairs={{0,8},{4,12},{8,0},{12,4},{16,24},{20,28},{24,16},{28,20},{1,9},{5... | collective-permute-start | bytes 1572872 | tf_op jit(solution)/shard_map/ppermute | solution.py:137
  226.1 32.9 %collective-permute-start.29 = (bf16[512,1024]{1,0:T(8,128)(2,1)}, bf16[512,1024]{1,0:T(8,128)(2,1)}, u32[]{:S(2)}, u32[]{:S(2)}) collective-permute-start(bf16[512,1024]{1,0:T(8,128)(2,1)} %bitcast.99), channel_id=1, source_target_pairs={{0,4},{4,0},{8,12},{12,8},{16,20},{20,16},{24,28},{28,24},{1,5},{5... | collective-permute-start | bytes 3145736 | tf_op jit(solution)/shard_map/ppermute | solution.py:137
  442.8 58.8 %collective-permute-start.72 = (bf16[512,1024]{1,0:T(8,128)(2,1)}, bf16[512,1024]{1,0:T(8,128)(2,1)S(1)}, u32[]{:S(2)}, u32[]{:S(2)}) collective-permute-start(bf16[512,1024]{1,0:T(8,128)(2,1)} %slice_bitcast_fusion.6), channel_id=1, source_target_pairs={{0,4},{4,0},{8,12},{12,8},{16,20},{20,16},{24,28},{28,24},{1,5},{5... | collective-permute-start | bytes 3145736 | tf_op jit(solution)/shard_map/ppermute | solution.py:137
  448.7 47.6 %collective-permute-start.81 = (bf16[512,1024]{1,0:T(8,128)(2,1)}, bf16[512,1024]{1,0:T(8,128)(2,1)}, u32[]{:S(2)}, u32[]{:S(2)}) collective-permute-start(bf16[512,1024]{1,0:T(8,128)(2,1)} %slice_bitcast_fusion), channel_id=1, source_target_pairs={{0,4},{4,0},{8,12},{12,8},{16,20},{20,16},{24,28},{28,24},{1,5},{5... | collective-permute-start | bytes 3145736 | tf_op jit(solution)/shard_map/ppermute | solution.py:137
  448.9 41.2 %collective-permute-start.36 = (bf16[512,768]{1,0:T(8,128)(2,1)}, bf16[512,768]{1,0:T(8,128)(2,1)}, u32[]{:S(2)}, u32[]{:S(2)}) collective-permute-start(bf16[512,768]{1,0:T(8,128)(2,1)} %slice_bitcast_fusion.22), channel_id=1, source_target_pairs={{0,4},{4,0},{8,12},{12,8},{16,20},{20,16},{24,28},{28,24},{1,5},{5... | collective-permute-start | bytes 2359304 | tf_op jit(solution)/shard_map/ppermute | solution.py:137
  449.4 42.9 %collective-permute-start.39 = (bf16[512,768]{1,0:T(8,128)(2,1)}, bf16[512,768]{1,0:T(8,128)(2,1)}, u32[]{:S(2)}, u32[]{:S(2)}) collective-permute-start(bf16[512,768]{1,0:T(8,128)(2,1)} %slice_bitcast_fusion.20), channel_id=1, source_target_pairs={{0,4},{4,0},{8,12},{12,8},{16,20},{20,16},{24,28},{28,24},{1,5},{5... | collective-permute-start | bytes 2359304 | tf_op jit(solution)/shard_map/ppermute | solution.py:137
  489.8 146.4 %reduce-scatter.5.cloned.1.call-start = ((), (), s32[]{:S(2)}) async-start(), calls=%async_computation.4 | async-start | bytes 983040 | tf_op jit(solution)/shard_map/reduce_scatter | solution.py:178
  511.3 63.1 %collective-permute-start.73 = (bf16[256,1024]{1,0:T(8,128)(2,1)}, bf16[256,1024]{1,0:T(8,128)(2,1)}, u32[]{:S(2)}, u32[]{:S(2)}) collective-permute-start(bf16[256,1024]{1,0:T(8,128)(2,1)} %slice_bitcast_fusion.26), channel_id=1, source_target_pairs={{0,16},{4,20},{8,24},{12,28},{16,0},{20,4},{24,8},{28,12},{1,17},{... | collective-permute-start | bytes 1572872 | tf_op jit(solution)/shard_map/ppermute | solution.py:137
  515.0 64.9 %collective-permute-start.82 = (bf16[256,1024]{1,0:T(8,128)(2,1)}, bf16[256,1024]{1,0:T(8,128)(2,1)}, u32[]{:S(2)}, u32[]{:S(2)}) collective-permute-start(bf16[256,1024]{1,0:T(8,128)(2,1)} %bitcast.283), channel_id=1, source_target_pairs={{0,8},{4,12},{8,0},{12,4},{16,24},{20,28},{24,16},{28,20},{1,9},{5... | collective-permute-start | bytes 1572872 | tf_op jit(solution)/shard_map/ppermute | solution.py:137
  523.2 54.1 %collective-permute-start.76 = (bf16[256,1024]{1,0:T(8,128)(2,1)}, bf16[256,1024]{1,0:T(8,128)(2,1)}, u32[]{:S(2)}, u32[]{:S(2)}) collective-permute-start(bf16[256,1024]{1,0:T(8,128)(2,1)} %slice_bitcast_fusion.24), channel_id=1, source_target_pairs={{0,16},{4,20},{8,24},{12,28},{16,0},{20,4},{24,8},{28,12},{1,17},{... | collective-permute-start | bytes 1572872 | tf_op jit(solution)/shard_map/ppermute | solution.py:137
  524.9 56.8 %collective-permute-start.79 = (bf16[256,1024]{1,0:T(8,128)(2,1)}, bf16[256,1024]{1,0:T(8,128)(2,1)}, u32[]{:S(2)}, u32[]{:S(2)}) collective-permute-start(bf16[256,1024]{1,0:T(8,128)(2,1)} %bitcast.274), channel_id=1, source_target_pairs={{0,8},{4,12},{8,0},{12,4},{16,24},{20,28},{24,16},{28,20},{1,9},{5... | collective-permute-start | bytes 1572872 | tf_op jit(solution)/shard_map/ppermute | solution.py:137
  574.3 68.1 %reduce-scatter.11.cloned.1.call-start = ((), (), s32[]{:S(2)}) async-start(), calls=%async_computation.7 | async-start | bytes 1310720 | tf_op jit(solution)/shard_map/reduce_scatter | solution.py:178
  577.3 38.2 %collective-permute-start.61 = (bf16[256,1024]{1,0:T(8,128)(2,1)}, bf16[256,1024]{1,0:T(8,128)(2,1)}, u32[]{:S(2)}, u32[]{:S(2)}) collective-permute-start(bf16[256,1024]{1,0:T(8,128)(2,1)} %slice_bitcast_fusion.30), channel_id=1, source_target_pairs={{0,16},{4,20},{8,24},{12,28},{16,0},{20,4},{24,8},{28,12},{1,17},{... | collective-permute-start | bytes 1572872 | tf_op jit(solution)/shard_map/ppermute | solution.py:137
  579.9 38.9 %collective-permute-start.70 = (bf16[256,1024]{1,0:T(8,128)(2,1)}, bf16[256,1024]{1,0:T(8,128)(2,1)}, u32[]{:S(2)}, u32[]{:S(2)}) collective-permute-start(bf16[256,1024]{1,0:T(8,128)(2,1)} %bitcast.247), channel_id=1, source_target_pairs={{0,8},{4,12},{8,0},{12,4},{16,24},{20,28},{24,16},{28,20},{1,9},{5... | collective-permute-start | bytes 1572872 | tf_op jit(solution)/shard_map/ppermute | solution.py:137
  615.5 55.0 %reduce-scatter.9.cloned.1.call-start = ((), (), s32[]{:S(2)}) async-start(), calls=%async_computation.6 | async-start | bytes 1310720 | tf_op jit(solution)/shard_map/reduce_scatter | solution.py:178
  (179 other events, 1666.3 us)
Sparse Core Ops, SparseCore 0:
  10.2 32.9 all-gather.6
  44.8 26.2 all-gather.10
  72.6 27.4 all-gather.8
  489.9 19.7 reduce-scatter.6
  574.4 23.2 reduce-scatter.4
  615.6 26.7 reduce-scatter.10
  644.6 25.7 reduce-scatter.8

commit v3 on v2

--- a/solution.py
+++ b/solution.py
@@ -261,8 +261,12 @@
         jnp.stack([b_out, gain_one, shift_one, b_back, gain_two, shift_two]).astype(jnp.float32)
     )
     b_out, gain_one, shift_one, b_back, gain_two, shift_two = [vectors[i] for i in range(6)]
-    bias_qv_all = lax.all_gather(b_qv, "tensor", axis=1, tiled=True).astype(jnp.float32)
-    bias_in_all = lax.all_gather(b_in, "tensor", axis=0, tiled=True).astype(jnp.float32)
+    biases = lax.all_gather(jnp.concatenate([b_qv.reshape(-1), b_in]), "tensor", axis=0)
+    biases = biases.astype(jnp.float32)
+    bias_qv_all = jnp.concatenate(
+        [biases[g, : 2 * part].reshape(2, part) for g in range(groups)], axis=1
+    )
+    bias_in_all = biases[:, 2 * part :].reshape(-1)
 
     qkv_parts = []
     for g in range(groups):

time: 688 us -> 689 us (level)
  waiting for transfers between devices: 201 us -> 211 us
  blocking collectives: 65 us -> 56 us
    all_gather x3, waiting for transfers between devices: 33.9 us -> 43.1 us  [gather(): stacked = lax.all_gather(weight, 'tensor', axis=0)]
    all_gather x2 -> x1, blocking collectives: 24.8 us -> 15.8 us  [body(): lax.all_gather(jnp.concatenate([b_qv.reshape(-1), b_in]), 'tensor', axis=0)]
    unnamed x270 -> x271, local copies, waits for them, and re-layouts: 24.8 us -> 25.5 us
where the time goes in v3:
time: 689 us; the launch traced here: 681 us
  waiting for transfers between devices  211 us (31%)
  matrix products  106 us (15%)
  other arithmetic  89.2 us (13%)
  local copies, waits for them, and re-layouts  79.8 us (12%)
  starting transfers between devices  78.9 us (11%)
  blocking collectives  56 us (8%)
  Pallas kernels  38.1 us (6%)
  between operations  22.1 us (3%)
    ppermute x84, waiting for transfers between devices, exchange(): return lax.ppermute(value, 'dp', [(i, i ^ 1 << bit) for i in range(size)])  136 us
    ppermute x84, starting transfers between devices, exchange(): return lax.ppermute(value, 'dp', [(i, i ^ 1 << bit) for i in range(size)])  78.3 us
    another operation x36, other arithmetic, gather(): held = jnp.stack([held.reshape(shape), other.reshape(shape)], axis=1)  54.6 us
    all_gather x3, waiting for transfers between devices, gather(): stacked = lax.all_gather(weight, 'tensor', axis=0)  43.1 us
    dot_general x16, matrix products, dot(): return jnp.dot(a, b, preferred_element_type=jnp.float32)  42.7 us
    psum x1, blocking collectives, body(): lax.psum((jnp.concatenate([early, grad_b_in.reshape(-1, width)], axis=0),...  40.2 us
    dot_general x16, matrix products, dot_tn(): return lax.dot_general(a, b, ROWS_TN, preferred_element_type=jnp.float32)  35.3 us
    reduce_scatter x4, waiting for transfers between devices, scatter(): lax.psum_scatter(stacked, 'tensor', scatter_dimension=0, tiled=True)  30.6 us
  transfers between devices with their start and end apart: 91, of which 32 were waited for; matrix products, arithmetic and copies ran while one was open for 23% of the time, Pallas kernels for 2%

profile of v3, /device:TPU:0, one launch (start us, length us, event | category | flops | bytes accessed | tf_op | source)
XLA Modules:
  0.0 681.1 jit_solution(4922737426756381099)
XLA Ops:
  17.3 15.8 %all-gather.4 = bf16[4,1,1536]{2,1,0:T(2,128)(2,1)S(1)} all-gather(bf16[1,1,1536]{2,1,0:T(2,128)(2,1)S(1)} %reshape.552), channel_id=3, replica_groups=mesh['dp'=8,'tensor'=4] {'tensor'}, dimensions={0}, use_global_device_ids=true | all-gather | bytes 15360 | tf_op jit(solution)/shard_map/all_gather | solution.py:264
  54.6 18.0 %all-gather.13.cloned.1.call-done = bf16[512,1024]{1,0:T(8,128)(2,1)} async-done(((bf16[128,1024]{1,0:T(8,128)(2,1)}), bf16[512,1024]{1,0:T(8,128)(2,1)}) %all-gather.13.cloned.1.call-update) | async-done | bytes 1048592 | tf_op jit(solution)/shard_map/all_gather | solution.py:145
  76.6 25.1 %all-gather.11.cloned.1.call-done = bf16[512,1024]{1,0:T(8,128)(2,1)} async-done(((bf16[128,1024]{1,0:T(8,128)(2,1)}), bf16[512,1024]{1,0:T(8,128)(2,1)}) %all-gather.11.cloned.1.call-update) | async-done | bytes 1048592 | tf_op jit(solution)/shard_map/all_gather | solution.py:145
  141.8 14.7 %collective-permute-done.12 = bf16[128,1024]{1,0:T(8,128)(2,1)S(1)} collective-permute-done((bf16[128,1024]{1,0:T(8,128)(2,1)}, bf16[128,1024]{1,0:T(8,128)(2,1)S(1)}, u32[]{:S(2)}, u32[]{:S(2)}) %collective-permute-start.12) | collective-permute-done | bytes 262176 | tf_op jit(solution)/shard_map/ppermute | solution.py:137
  176.1 6.9 %collective-permute-done.13 = bf16[256,1024]{1,0:T(8,128)(2,1)} collective-permute-done((bf16[256,1024]{1,0:T(8,128)(2,1)}, bf16[256,1024]{1,0:T(8,128)(2,1)}, u32[]{:S(2)}, u32[]{:S(2)}) %collective-permute-start.13) | collective-permute-done | bytes 524320 | tf_op jit(solution)/shard_map/ppermute | solution.py:137
  188.3 4.1 collective-permute-done.31
  235.9 15.4 %shard_map.281 = bf16[512,1024]{1,0:T(8,128)(2,1)} custom-call(s32[1]{0:T(128)} %dynamic_slice.233.limit_ref, bf16[512,3072]{1,0:T(8,128)(2,1)} %pad_maximum_fusion.qkv_ref), custom_call_target="tpu_custom_call" | custom-call | flops 4294967296 | bytes 4194304 | tf_op jit(solution)/shard_map/pallas_call | solution.py:89
  264.3 6.6 fusion.17
  270.9 6.6 fusion.11
  279.6 6.8 fusion.8
  288.3 6.6 fusion.14
  321.9 22.7 %shard_map.282 = bf16[512,3072]{1,0:T(8,128)(2,1)} custom-call(s32[1]{0:T(128)} %dynamic_slice.233.limit_ref, bf16[512,3072]{1,0:T(8,128)(2,1)} %pad_maximum_fusion.qkv_ref, bf16[512,1024]{1,0:T(8,128)(2,1)} %pad_maximum_fusion.25.grad_ref), custom_call_target="tpu_custom_call" | custom-call | flops 10737418240 | bytes 7340032 | tf_op jit(solution)/shard_map/pallas_call | solution.py:109
  344.7 4.1 fusion.70
  389.8 40.2 %all-reduce = (f32[2,1024]{1,0:T(2,128)S(1)}, f32[10,1024]{1,0:T(8,128)S(1)}) all-reduce(f32[2,1024]{1,0:T(2,128)S(1)} %pad_maximum_fusion.49, f32[10,1024]{1,0:T(8,128)S(1)} %pad_maximum_fusion.43), channel_id=1, replica_groups=mesh['dp'=8,'tensor'=4] {'dp','tensor'}, use_global_device_ids=true, to_apply=%region_10.0 | all-reduce | flops 12288 | bytes 98304 | tf_op jit(solution)/shard_map/psum | solution.py:346
  453.6 4.0 collective-permute-done.58
  469.4 4.1 collective-permute-done.52
  518.0 6.8 collective-permute-done.40
  531.4 24.3 %collective-permute-done.38 = bf16[128,768]{1,0:T(8,128)(2,1)S(1)} collective-permute-done((bf16[128,768]{1,0:T(8,128)(2,1)S(1)}, bf16[128,768]{1,0:T(8,128)(2,1)S(1)}, u32[]{:S(2)}, u32[]{:S(2)}) %collective-permute-start.38) | collective-permute-done | bytes 196640 | tf_op jit(solution)/shard_map/ppermute | solution.py:137
  557.3 4.7 collective-permute-done.41
  562.3 5.3 collective-permute-done.47
  568.1 6.1 collective-permute-done.44
  594.5 12.8 %collective-permute-done.74 = bf16[128,1024]{1,0:T(8,128)(2,1)S(1)} collective-permute-done((bf16[128,1024]{1,0:T(8,128)(2,1)S(1)}, bf16[128,1024]{1,0:T(8,128)(2,1)S(1)}, u32[]{:S(2)}, u32[]{:S(2)}) %collective-permute-start.74) | collective-permute-done | bytes 262176 | tf_op jit(solution)/shard_map/ppermute | solution.py:137
  639.7 4.2 reduce-scatter.11.cloned.1.call-done
  645.7 26.3 %reduce-scatter.9.cloned.1.call-done = bf16[128,1024]{1,0:T(8,128)(2,1)} async-done(((bf16[512,1024]{1,0:T(8,128)(2,1)}), bf16[128,1024]{1,0:T(8,128)(2,1)}) %reduce-scatter.9.cloned.1.call-update) | async-done | bytes 262160 | tf_op jit(solution)/shard_map/reduce_scatter | solution.py:178
  (691 shorter events, 366.6 us)
Async XLA Ops:
  7.2 41.0 %all-gather.9.cloned.1.call-start = ((), (), s32[]{:S(2)}) async-start(), calls=%async_computation.8 | async-start | bytes 1310720 | tf_op jit(solution)/shard_map/all_gather | solution.py:145
  10.1 62.5 %all-gather.13.cloned.1.call-start = ((), (), s32[]{:S(2)}) async-start(), calls=%async_computation.10 | async-start | bytes 1310720 | tf_op jit(solution)/shard_map/all_gather | solution.py:145
  10.9 90.8 %all-gather.11.cloned.1.call-start = ((), (), s32[]{:S(2)}) async-start(), calls=%async_computation.9 | async-start | bytes 1310720 | tf_op jit(solution)/shard_map/all_gather | solution.py:145
  11.6 624.6 %reduce-scatter.7.cloned.1.call-start = ((), (), s32[]{:S(2)}) async-start(), calls=%async_computation.5 | async-start | bytes 327680 | tf_op jit(solution)/shard_map/reduce_scatter | solution.py:178
  50.5 56.8 %collective-permute-start.6 = (bf16[128,1024]{0,1:T(8,128)(2,1)S(1)}, bf16[128,1024]{0,1:T(8,128)(2,1)}, u32[]{:S(2)}, u32[]{:S(2)}) collective-permute-start(bf16[128,1024]{0,1:T(8,128)(2,1)S(1)} %get-tuple-element.100), channel_id=1, source_target_pairs={{0,16},{4,20},{8,24},{12,28},{16,0},{20,4},{24,8},{28,12},{1,17},{... | collective-permute-start | bytes 786440 | tf_op jit(solution)/shard_map/ppermute | solution.py:137
  52.1 74.2 %collective-permute-start.3 = (bf16[128,1024]{0,1:T(8,128)(2,1)}, bf16[128,1024]{0,1:T(8,128)(2,1)}, u32[]{:S(2)}, u32[]{:S(2)}) collective-permute-start(bf16[128,1024]{0,1:T(8,128)(2,1)} %get-tuple-element.101), channel_id=1, source_target_pairs={{0,8},{4,12},{8,0},{12,4},{16,24},{20,28},{24,16},{28,20},{1,9},{5... | collective-permute-start | bytes 786440 | tf_op jit(solution)/shard_map/ppermute | solution.py:137
  53.6 68.3 %collective-permute-start = (bf16[128,1024]{0,1:T(8,128)(2,1)}, bf16[128,1024]{0,1:T(8,128)(2,1)}, u32[]{:S(2)}, u32[]{:S(2)}) collective-permute-start(bf16[128,1024]{0,1:T(8,128)(2,1)} %get-tuple-element.102), channel_id=1, source_target_pairs={{0,8},{4,12},{8,0},{12,4},{16,24},{20,28},{24,16},{28,20},{1,9},{5... | collective-permute-start | bytes 786440 | tf_op jit(solution)/shard_map/ppermute | solution.py:137
  54.1 49.9 %collective-permute-start.9 = (bf16[128,1024]{0,1:T(8,128)(2,1)}, bf16[128,1024]{0,1:T(8,128)(2,1)}, u32[]{:S(2)}, u32[]{:S(2)}) collective-permute-start(bf16[128,1024]{0,1:T(8,128)(2,1)} %get-tuple-element.103), channel_id=1, source_target_pairs={{0,16},{4,20},{8,24},{12,28},{16,0},{20,4},{24,8},{28,12},{1,17},{... | collective-permute-start | bytes 786440 | tf_op jit(solution)/shard_map/ppermute | solution.py:137
  75.1 39.6 %collective-permute-start.27 = (bf16[128,1024]{1,0:T(8,128)(2,1)}, bf16[128,1024]{1,0:T(8,128)(2,1)}, u32[]{:S(2)}, u32[]{:S(2)}) collective-permute-start(bf16[128,1024]{1,0:T(8,128)(2,1)} %get-tuple-element.84), channel_id=1, source_target_pairs={{0,16},{4,20},{8,24},{12,28},{16,0},{20,4},{24,8},{28,12},{1,17},{... | collective-permute-start | bytes 786440 | tf_op jit(solution)/shard_map/ppermute | solution.py:137
  128.0 32.5 %collective-permute-start.10 = (bf16[256,1024]{1,0:T(8,128)(2,1)}, bf16[256,1024]{1,0:T(8,128)(2,1)}, u32[]{:S(2)}, u32[]{:S(2)}) collective-permute-start(bf16[256,1024]{1,0:T(8,128)(2,1)} %bitcast.706), channel_id=1, source_target_pairs={{0,8},{4,12},{8,0},{12,4},{16,24},{20,28},{24,16},{28,20},{1,9},{5... | collective-permute-start | bytes 1572872 | tf_op jit(solution)/shard_map/ppermute | solution.py:137
  227.7 32.9 %collective-permute-start.29 = (bf16[512,1024]{1,0:T(8,128)(2,1)}, bf16[512,1024]{1,0:T(8,128)(2,1)}, u32[]{:S(2)}, u32[]{:S(2)}) collective-permute-start(bf16[512,1024]{1,0:T(8,128)(2,1)} %bitcast.102), channel_id=1, source_target_pairs={{0,4},{4,0},{8,12},{12,8},{16,20},{20,16},{24,28},{28,24},{1,5},{5... | collective-permute-start | bytes 3145736 | tf_op jit(solution)/shard_map/ppermute | solution.py:137
  444.4 58.8 %collective-permute-start.72 = (bf16[512,1024]{1,0:T(8,128)(2,1)}, bf16[512,1024]{1,0:T(8,128)(2,1)S(1)}, u32[]{:S(2)}, u32[]{:S(2)}) collective-permute-start(bf16[512,1024]{1,0:T(8,128)(2,1)} %slice_bitcast_fusion.6), channel_id=1, source_target_pairs={{0,4},{4,0},{8,12},{12,8},{16,20},{20,16},{24,28},{28,24},{1,5},{5... | collective-permute-start | bytes 3145736 | tf_op jit(solution)/shard_map/ppermute | solution.py:137
  450.2 47.6 %collective-permute-start.81 = (bf16[512,1024]{1,0:T(8,128)(2,1)}, bf16[512,1024]{1,0:T(8,128)(2,1)}, u32[]{:S(2)}, u32[]{:S(2)}) collective-permute-start(bf16[512,1024]{1,0:T(8,128)(2,1)} %slice_bitcast_fusion), channel_id=1, source_target_pairs={{0,4},{4,0},{8,12},{12,8},{16,20},{20,16},{24,28},{28,24},{1,5},{5... | collective-permute-start | bytes 3145736 | tf_op jit(solution)/shard_map/ppermute | solution.py:137
  450.4 41.2 %collective-permute-start.36 = (bf16[512,768]{1,0:T(8,128)(2,1)}, bf16[512,768]{1,0:T(8,128)(2,1)}, u32[]{:S(2)}, u32[]{:S(2)}) collective-permute-start(bf16[512,768]{1,0:T(8,128)(2,1)} %slice_bitcast_fusion.22), channel_id=1, source_target_pairs={{0,4},{4,0},{8,12},{12,8},{16,20},{20,16},{24,28},{28,24},{1,5},{5... | collective-permute-start | bytes 2359304 | tf_op jit(solution)/shard_map/ppermute | solution.py:137
  450.9 42.9 %collective-permute-start.39 = (bf16[512,768]{1,0:T(8,128)(2,1)}, bf16[512,768]{1,0:T(8,128)(2,1)}, u32[]{:S(2)}, u32[]{:S(2)}) collective-permute-start(bf16[512,768]{1,0:T(8,128)(2,1)} %slice_bitcast_fusion.20), channel_id=1, source_target_pairs={{0,4},{4,0},{8,12},{12,8},{16,20},{20,16},{24,28},{28,24},{1,5},{5... | collective-permute-start | bytes 2359304 | tf_op jit(solution)/shard_map/ppermute | solution.py:137
  491.3 146.4 %reduce-scatter.5.cloned.1.call-start = ((), (), s32[]{:S(2)}) async-start(), calls=%async_computation.4 | async-start | bytes 983040 | tf_op jit(solution)/shard_map/reduce_scatter | solution.py:178
  512.8 63.1 %collective-permute-start.73 = (bf16[256,1024]{1,0:T(8,128)(2,1)}, bf16[256,1024]{1,0:T(8,128)(2,1)}, u32[]{:S(2)}, u32[]{:S(2)}) collective-permute-start(bf16[256,1024]{1,0:T(8,128)(2,1)} %slice_bitcast_fusion.26), channel_id=1, source_target_pairs={{0,16},{4,20},{8,24},{12,28},{16,0},{20,4},{24,8},{28,12},{1,17},{... | collective-permute-start | bytes 1572872 | tf_op jit(solution)/shard_map/ppermute | solution.py:137
  516.5 64.9 %collective-permute-start.82 = (bf16[256,1024]{1,0:T(8,128)(2,1)}, bf16[256,1024]{1,0:T(8,128)(2,1)}, u32[]{:S(2)}, u32[]{:S(2)}) collective-permute-start(bf16[256,1024]{1,0:T(8,128)(2,1)} %bitcast.287), channel_id=1, source_target_pairs={{0,8},{4,12},{8,0},{12,4},{16,24},{20,28},{24,16},{28,20},{1,9},{5... | collective-permute-start | bytes 1572872 | tf_op jit(solution)/shard_map/ppermute | solution.py:137
  524.8 54.1 %collective-permute-start.76 = (bf16[256,1024]{1,0:T(8,128)(2,1)}, bf16[256,1024]{1,0:T(8,128)(2,1)}, u32[]{:S(2)}, u32[]{:S(2)}) collective-permute-start(bf16[256,1024]{1,0:T(8,128)(2,1)} %slice_bitcast_fusion.24), channel_id=1, source_target_pairs={{0,16},{4,20},{8,24},{12,28},{16,0},{20,4},{24,8},{28,12},{1,17},{... | collective-permute-start | bytes 1572872 | tf_op jit(solution)/shard_map/ppermute | solution.py:137
  526.4 56.8 %collective-permute-start.79 = (bf16[256,1024]{1,0:T(8,128)(2,1)}, bf16[256,1024]{1,0:T(8,128)(2,1)}, u32[]{:S(2)}, u32[]{:S(2)}) collective-permute-start(bf16[256,1024]{1,0:T(8,128)(2,1)} %bitcast.278), channel_id=1, source_target_pairs={{0,8},{4,12},{8,0},{12,4},{16,24},{20,28},{24,16},{28,20},{1,9},{5... | collective-permute-start | bytes 1572872 | tf_op jit(solution)/shard_map/ppermute | solution.py:137
  575.8 68.1 %reduce-scatter.11.cloned.1.call-start = ((), (), s32[]{:S(2)}) async-start(), calls=%async_computation.7 | async-start | bytes 1310720 | tf_op jit(solution)/shard_map/reduce_scatter | solution.py:178
  578.9 38.2 %collective-permute-start.61 = (bf16[256,1024]{1,0:T(8,128)(2,1)}, bf16[256,1024]{1,0:T(8,128)(2,1)}, u32[]{:S(2)}, u32[]{:S(2)}) collective-permute-start(bf16[256,1024]{1,0:T(8,128)(2,1)} %slice_bitcast_fusion.30), channel_id=1, source_target_pairs={{0,16},{4,20},{8,24},{12,28},{16,0},{20,4},{24,8},{28,12},{1,17},{... | collective-permute-start | bytes 1572872 | tf_op jit(solution)/shard_map/ppermute | solution.py:137
  581.5 38.9 %collective-permute-start.70 = (bf16[256,1024]{1,0:T(8,128)(2,1)}, bf16[256,1024]{1,0:T(8,128)(2,1)}, u32[]{:S(2)}, u32[]{:S(2)}) collective-permute-start(bf16[256,1024]{1,0:T(8,128)(2,1)} %bitcast.251), channel_id=1, source_target_pairs={{0,8},{4,12},{8,0},{12,4},{16,24},{20,28},{24,16},{28,20},{1,9},{5... | collective-permute-start | bytes 1572872 | tf_op jit(solution)/shard_map/ppermute | solution.py:137
  617.0 55.0 %reduce-scatter.9.cloned.1.call-start = ((), (), s32[]{:S(2)}) async-start(), calls=%async_computation.6 | async-start | bytes 1310720 | tf_op jit(solution)/shard_map/reduce_scatter | solution.py:178
  (178 other events, 1656.1 us)
Sparse Core Ops, SparseCore 0:
  10.2 33.0 all-gather.8
  44.9 27.6 all-gather.12
  74.2 27.4 all-gather.10
  491.4 19.7 reduce-scatter.6
  576.0 23.2 reduce-scatter.4
  617.2 26.7 reduce-scatter.10
  646.2 25.7 reduce-scatter.8
